TPU v7x, 128 devices: a whole 4x4x4 slice. The times are simulated.
128 devices in a mesh: tm: 2 (over x_lo), gz: 8 (over y, x_hi), view: 8 (over z, core).
Axes of the slice: x: 4 (x_hi: 2, x_lo: 2; x = x_hi * 2 + x_lo), y: 4, z: 4, core: 2. Of those that a mesh axis runs over, the one named last changes fastest.
Arguments:
- sinogram: bfloat16 [2, 16, 1024, 2560], P(None, 'view', ('tm', 'gz')), may hold values from 102 to 358
- projector: bfloat16 [16, 1024, 2560], P('view'), may hold values from 0.0099487305 to 1
- warm_volume: float32 [1024, 1024], P(('tm', 'gz')), may hold values from 0.2 to 2.5, as said below
- view_order: int32 [2], replicated, may hold values from 0 to 1, each once
Outputs:
- volumes: float32 [2, 1024, 1024], P(None, ('tm', 'gz'))
Inputs may be any that keep to these rules, and one draw needn't show every extreme that they name: `view_order`: each local view number appears once. `warm_volume`: positive attenuation values.
All inputs are finite; a program needn't handle non-finite values.
Results may differ from a plain program's by a relative error of at most 0.0003.
Values may be sent and summed in bfloat16 or wider, within the bound.
No kernel may reach another device: no remote copies, remote signals or barrier semaphores. Data moves between devices by JAX's collectives and lax.ppermute only.
A program may use at most 64 MiB of HBM per device.

v0:
```python
import functools

import jax
import jax.numpy as jnp
from jax import lax
from jax.experimental import pallas as pl
from jax.experimental.pallas import tpu as pltpu
from jax.sharding import PartitionSpec as P

RY = 128
FRAMES = 2
SWEEPS = 3
TV_STEPS = 2
HALO = 16
CHUNK = 1280
ROWS = 32
QUARTERS = 4
AXES = ("tm", "gz", "view")

RELAXATION = 0.9
STEP_SCALE = 0.3
STEP_DECAY = 0.7
SMOOTHING = 0.01
NORM_GUARD = 1e-06

F32 = jnp.float32
BF16 = jnp.bfloat16
WHOLE = pl.BlockSpec(memory_space=pltpu.VMEM)
SCALARS = pl.BlockSpec(memory_space=pltpu.SMEM)


def params(mib):
    return pltpu.CompilerParams(vmem_limit_bytes=mib * 1024 * 1024)


def near(array):
    return pltpu.with_memory_space_constraint(array, pltpu.VMEM)


def call(kernel, outs, ids, *arrays, scratch=()):
    return pl.pallas_call(
        kernel,
        out_shape=tuple(pltpu.VMEM(shape, dtype) for shape, dtype in outs),
        in_specs=[SCALARS] + [WHOLE] * len(arrays),
        out_specs=tuple(WHOLE for _ in outs),
        scratch_shapes=scratch,
        compiler_params=params(12),
    )(ids, *[near(a) for a in arrays])


def keeps(d):
    return d[4] == d[1] // 2


def move(array, rule, source=None):
    pairs = []
    for tm in range(2):
        for y in range(4):
            for h in range(2):
                for z in range(4):
                    for c in range(2):
                        here = (tm, y, h, z, c)
                        if source is not None and not source(here):
                            continue
                        there = rule(*here)
                        if there is None:
                            continue
                        index = [((t * 4 + a) * 2 + b) * 8 + 2 * u + v for t, a, b, u, v in (here, there)]
                        pairs.append(tuple(index))
    return lax.ppermute(array, AXES, pairs)


def after(array, *others):
    return lax.optimization_barrier((array, *others))[0]


def flip(dtm=0, dy=0, dh=0, dz=0, dc=0):
    return lambda tm, y, h, z, c: (tm ^ dtm, y ^ dy, h ^ dh, z ^ dz, c ^ dc)


def strip_step(step):
    def rule(tm, y, h, z, c):
        strip = 2 * tm + c + step
        return (strip // 2, y, h, z, strip % 2) if 0 <= strip < 4 else None

    return rule


def gram_kernel(ids_ref, a_ref, s0_ref, s1_ref, own_ref, send_ref, acc, level_ref):
    n = pl.program_id(0)
    rows, det = s0_ref.shape
    my_rows = pl.ds(pl.multiple_of(ids_ref[1] * rows, rows), rows)

    acc[...] = jnp.zeros_like(acc)

    def chunk(d, carry):
        at = pl.ds(pl.multiple_of(d * CHUNK, CHUNK), CHUNK)
        tile = a_ref[:, at]
        ray = jnp.sum(tile.astype(F32), axis=0, keepdims=True)
        inverse = 1.0 / ray
        lhs = []
        for t, ref in enumerate((s0_ref, s1_ref)):
            scaled = ref[:, at].astype(F32) * inverse

            @pl.when(d == 0)
            def _():
                mean = jnp.sum(scaled, axis=1, keepdims=True) / CHUNK
                level_ref[t] = jnp.broadcast_to(mean, level_ref.shape[1:])

            lhs.append((scaled - level_ref[t, :, 0:1]).astype(BF16))
        lhs.append((a_ref[my_rows, at].astype(F32) * inverse).astype(BF16))
        lhs.append(jnp.ones((16, CHUNK), BF16))
        stack = jnp.concatenate(lhs, axis=0)
        acc[...] += lax.dot_general(stack, tile, (((1,), (1,)), ((), ())), preferred_element_type=F32)
        return carry

    lax.fori_loop(0, det // CHUNK, chunk, 0)

    part = rows // QUARTERS
    at = pl.ds(pl.multiple_of(n * part, part), part)
    for t in range(FRAMES):
        for ref, who in ((own_ref, 1 - t), (send_ref, t)):

            @pl.when(ids_ref[4] == who)
            def _():
                for quarter in range(QUARTERS):
                    lo = quarter * part
                    ref[jnp.bitwise_xor(ids_ref[2], quarter), at, :] = (
                        acc[t * rows + lo : t * rows + lo + part]
                        + level_ref[t, lo : lo + part, 0:1] * acc[3 * rows : 3 * rows + 1]
                    )

    for ref, mine_too in ((own_ref, True), (send_ref, False)):

        @pl.when((ids_ref[3] == n) == mine_too)
        def _():
            for quarter in range(QUARTERS):
                lo = 2 * rows + quarter * part
                ref[jnp.bitwise_xor(ids_ref[2], quarter), 2 * part : 3 * part, :] = acc[lo : lo + part]

        for half in range(2):

            @pl.when(n == half)
            def _():
                cover = acc[3 * rows : 3 * rows + 8]
                for k in range(QUARTERS):
                    ref[k, 3 * part + half : 3 * part + 8, :] = cover[half:8]


def gram_products(ids, projector, measured):
    _, pixels, det = projector.shape
    rows = measured.shape[2]
    part = rows // QUARTERS
    shape = (QUARTERS, 3 * part + 8, pixels)
    out = pl.BlockSpec(shape, lambda n, s: (0, 0, 0))
    projector = pltpu.with_memory_space_constraint(projector, pltpu.HBM)
    measured = pltpu.with_memory_space_constraint(measured, pltpu.HBM)
    return pl.pallas_call(
        gram_kernel,
        out_shape=(jax.ShapeDtypeStruct(shape, F32),) * 2,
        grid_spec=pltpu.PrefetchScalarGridSpec(
            num_scalar_prefetch=1,
            grid=(2,),
            in_specs=[
                pl.BlockSpec((None, pixels, det), lambda n, s: (s[8 + n], 0, 0)),
                pl.BlockSpec((None, None, rows, det), lambda n, s: (0, s[8 + n], 0, 0)),
                pl.BlockSpec((None, None, rows, det), lambda n, s: (1, s[8 + n], 0, 0)),
            ],
            out_specs=(out, out),
            scratch_shapes=[pltpu.VMEM((3 * rows + 16, pixels), F32), pltpu.VMEM((FRAMES, rows, RY), F32)],
        ),
        compiler_params=params(24),
        name="gram_products",
    )(ids, projector, measured, measured)


def chip_sum_kernel(ids_ref, own_ref, got_ref, *outs):
    for k, out in enumerate(outs):
        out[...] = own_ref[k] + got_ref[k]


def reduce_kernel(ids_ref, a0, a1, a2, a3, b_ref, gram_ref, aux_ref):
    part = gram_ref.shape[0]
    total = (a0[...] + a1[...]) + (a2[...] + a3[...])
    cov = total[3 * part : 3 * part + 8]
    scale = RELAXATION / cov
    share = cov / jnp.sum(cov, axis=1, keepdims=True)
    for n in range(2):
        b_ref[n] = total[n * part : (n + 1) * part] * scale[n : n + 1]
        aux_ref[n : n + 1] = RELAXATION * share[n : n + 1]
        aux_ref[2 + n : 3 + n] = scale[n : n + 1]
    rows = total[2 * part : 3 * part]
    own = jnp.sum(rows, axis=1, keepdims=True)
    mine = jnp.where(ids_ref[3] == 0, share[0:1], share[1:2])
    gram_ref[...] = (rows - own * mine).astype(BF16)


def place_gram_kernel(ids_ref, y0, y1, y2, y3, out_ref):
    z, y, h, tm = ids_ref[2], ids_ref[5], ids_ref[6], ids_ref[7]
    part = y0.shape[1]
    for dy, ref in enumerate((y0, y1, y2, y3)):

        def place(dx, carry):
            slab = (
                jnp.bitwise_xor(tm, dx // 2) * 8
                + jnp.bitwise_xor(y, dy) * 2
                + jnp.bitwise_xor(h, dx % 2)
            )
            for k in range(QUARTERS):
                row = slab * (QUARTERS * part) + jnp.bitwise_xor(z, k) * part
                out_ref[pl.ds(pl.multiple_of(row, part), part), :] = ref[dx * QUARTERS + k]
            return carry

        lax.fori_loop(0, 4, place, 0)


def place_rows_kernel(ids_ref, z0, z1, z2, z3, out_ref, head_ref, tail_ref):
    z = ids_ref[2]
    part = z0.shape[2]
    for k, ref in enumerate((z0, z1, z2, z3)):
        start = jnp.bitwise_xor(z, k) * part

        def place(slab, carry):
            row = slab * (QUARTERS * part) + start
            for n in range(2):
                out_ref[n, pl.ds(pl.multiple_of(row, part), part), :] = ref[slab, n]
            return carry

        lax.fori_loop(0, 4, place, 0)
    head_ref[...] = out_ref[:, :HALO]
    tail_ref[...] = out_ref[:, out_ref.shape[1] - HALO :]


def tv_into(x_ref, g_ref, ss_ref, flux_ref, first, depth):
    height, pixels = x_ref.shape
    blocks = pixels // RY

    @pl.when(first < 0)
    def _():
        x_ref[HALO - 1 : HALO, :] = x_ref[HALO : HALO + 1, :]

    @pl.when(first + height > depth)
    def _():
        x_ref[height - HALO : height - HALO + 1, :] = x_ref[height - HALO - 1 : height - HALO, :]

    column = (lax.broadcasted_iota(jnp.int32, (ROWS, RY), 1) < RY - 1).astype(F32)
    flux_ref[...] = jnp.zeros_like(flux_ref)

    def block(i, folded):
        here_at = pl.ds(pl.multiple_of(i * RY, RY), RY)
        next_at = pl.ds(pl.multiple_of(jnp.minimum(i + 1, blocks - 1) * RY, RY), RY)
        above = jnp.zeros((8, RY), F32)
        for lo in range(0, height, ROWS):
            hi = lo + ROWS
            here = x_ref[lo:hi, here_at]
            tail = x_ref[hi : hi + 8, here_at] if hi < height else here[ROWS - 8 :]
            below = pltpu.roll(jnp.concatenate([here, tail]), ROWS + 7, 0)[:ROWS]
            dz = below - here
            dc = (pltpu.roll(here, RY - 1, 1) - here) * column
            di = x_ref[lo:hi, next_at] - here
            square = dz * dz + dc * dc + di * di + SMOOTHING
            r = lax.rsqrt(square)
            r = r * (1.5 - (0.5 * square) * (r * r))
            fz = dz * r
            fc = dc * r
            fi = di * r
            over = pltpu.roll(jnp.concatenate([above, fz]), 1, 0)[8:]
            above = fz[ROWS - 8 :]
            g = (over - fz) + (flux_ref[lo:hi] - fi) + (pltpu.roll(fc, 1, 1) - fc)
            flux_ref[lo:hi] = fi
            g_ref[lo:hi, here_at] = g
            for k in range(0, ROWS, 8):
                if HALO <= lo + k < height - HALO:
                    folded = folded + g[k : k + 8] * g[k : k + 8]
        return folded

    ss_ref[...] = lax.fori_loop(0, blocks, block, jnp.zeros((8, RY), F32), unroll=2)


def descend(x_ref, g_ref, sums, step, cells, x_out):
    folded = (sums[0][...] + sums[1][...]) + (sums[2][...] + sums[3][...])
    total = jnp.sum(folded, axis=(0, 1), keepdims=True)
    factor = (STEP_SCALE * STEP_DECAY**step) / jnp.sqrt(total / cells + NORM_GUARD)
    chunk = x_ref.shape[0] // 3

    def rows(k, carry):
        at = pl.ds(pl.multiple_of(k * chunk, 8), chunk)
        x_out[at, :] = x_ref[at, :] - factor * g_ref[at, :]
        return carry

    lax.fori_loop(0, 3, rows, 0)


def first_kernel(ids_ref, x_ref, x_out, g_ref, ss_ref, flux, *, depth):
    x_out[...] = x_ref[...]
    tv_into(x_out, g_ref, ss_ref, flux, ids_ref[0], depth)


def second_kernel(ids_ref, x_ref, g_ref, s0, s1, s2, s3, x_out, g_out, ss_out, flux, *, depth, step, cells):
    descend(x_ref, g_ref, (s0, s1, s2, s3), step, cells, x_out)
    tv_into(x_out, g_out, ss_out, flux, ids_ref[0], depth)


def subset_kernel(
    ids_ref, x_ref, g_ref, s0, s1, s2, s3, mine_ref, other_ref, low_ref, b_ref, high_ref, aux_ref, *rest, depth, step, cells, last, final
):
    flux, product = rest[-2:]
    x_out = rest[0]
    height = x_ref.shape[0]
    parts = ((low_ref, 0, HALO), (b_ref, HALO, height - HALO), (high_ref, height - HALO, height))
    descend(x_ref, g_ref, (s0, s1, s2, s3), step, cells, x_out)
    core = ids_ref[3]

    def subset(n, carry):
        rounded = x_out[...].astype(BF16)

        @pl.when(n == core)
        def _():
            product[...] = jnp.dot(rounded, mine_ref[...], preferred_element_type=F32)

        @pl.when(n != core)
        def _():
            product[...] = jnp.dot(rounded, other_ref[...], preferred_element_type=F32)

        along = jnp.sum(rounded.astype(F32) * aux_ref[pl.ds(n, 1), :], axis=1, keepdims=True)
        scale = aux_ref[pl.ds(2 + n, 1), :]
        for ref, lo, hi in parts:
            change = ref[n] - product[lo:hi] * scale - along[lo:hi]
            x_out[lo:hi] = jnp.maximum(x_out[lo:hi] + change, 0.0)
        return carry

    lax.fori_loop(0, 2, subset, 0)
    if last:
        slab_out = rest[1]
        rows = slab_out.shape[0]
        start = HALO + jnp.bitwise_and(ids_ref[1], 3) * rows
        slab_out[...] = x_out[pl.ds(pl.multiple_of(start, HALO), rows), :]
    if not final:
        g_out, ss_out = rest[1 + last : 3 + last]
        tv_into(x_out, g_out, ss_out, flux, ids_ref[0], depth)


def body(sinogram, projector, warm_volume, view_order):
    slices, pixels = warm_volume.shape
    part = slices // QUARTERS
    tm = lax.axis_index("tm").astype(jnp.int32)
    gz = lax.axis_index("gz").astype(jnp.int32)
    view = lax.axis_index("view").astype(jnp.int32)
    y, h = gz // 2, gz % 2
    z, c = view // 2, view % 2
    slab = tm * 8 + gz
    keeper = c == y // 2
    depth = slices * 16
    cells = depth * pixels
    inner = 4 * slices
    height = inner + 2 * HALO
    first = (2 * tm + c) * inner - HALO
    ids = jnp.stack([first, slab, z, c, keeper.astype(jnp.int32), y, h, tm])
    ids = jnp.concatenate([ids, view_order])

    def pair_of(unit):
        across = move(unit, flip(dh=1))
        return jnp.where(h == 0, jnp.stack([unit, across]), jnp.stack([across, unit]))

    def strip_of(pair):
        one, two, three = (move(pair, flip(dy=k), keeps) for k in range(1, 4))
        same = jnp.where(keeper, pair, two)
        flipped = jnp.where(keeper, one, three)
        return jnp.where(
            y % 2 == 0, jnp.concatenate([same, flipped]), jnp.concatenate([flipped, same])
        )

    def widen(array, dim):
        length = array.shape[dim]
        low = move(lax.slice_in_dim(array, length - HALO, length, axis=dim), strip_step(1))
        high = move(lax.slice_in_dim(array, 0, HALO, axis=dim), strip_step(-1))
        return jnp.concatenate([low, array, high], axis=dim)

    own, send = gram_products(ids, projector, sinogram)
    passed = move(send, flip(dc=1))
    warm_pair = pair_of(after(warm_volume, send))
    block = (own.shape[1:], F32)
    terms = call(chip_sum_kernel, [block] * QUARTERS, ids, own, passed)
    terms = [terms[0]] + [move(terms[k], flip(dz=k)) for k in range(1, QUARTERS)]
    b_unit, piece, aux = call(
        reduce_kernel,
        [((2, part, pixels), F32), ((part, pixels), BF16), ((8, pixels), F32)],
        ids,
        *terms,
    )

    line = jnp.stack([piece] + [move(piece, flip(dz=k)) for k in range(1, 4)])
    flips = (flip(dh=1), flip(dtm=1), flip(dtm=1, dh=1))
    plane = jnp.concatenate([line] + [move(line, f) for f in flips])
    spread = [move(plane, flip(dy=k)) for k in range(1, 4)]

    def along_z(strip):
        return [strip] + [move(strip, flip(dz=k)) for k in range(1, 4)]

    def b_rows(quarters):
        edge = ((2, HALO, pixels), F32)
        rows, head, tail = call(
            place_rows_kernel, [((2, inner, pixels), F32), edge, edge], ids, *quarters
        )
        return move(tail, strip_step(1)), rows, move(head, strip_step(-1))

    strip = strip_of(pair_of(b_unit))
    quarters = along_z(strip)
    later = move(after(b_unit, strip), flip(dc=1), lambda d: not keeps(d))
    later = along_z(strip_of(pair_of(later)))

    big = ((height, pixels), F32)
    small = ((8, RY), F32)
    flux = pltpu.VMEM((height, RY), F32)

    def everyone(sums):
        flips = (flip(dc=1), flip(dtm=1), flip(dtm=1, dc=1))
        return [sums] + [move(sums, f) for f in flips]

    x = widen(strip_of(after(warm_pair, terms[0])).reshape(inner, pixels), 0)
    x = after(x, strip)
    x, g, sums = call(
        functools.partial(first_kernel, depth=depth), [big, big, small], ids, x, scratch=[flux]
    )
    b_wide = [None, None]
    finished = []
    for frame in range(FRAMES):
        for sweep in range(SWEEPS):
            step = sweep * TV_STEPS
            x, g, sums = call(
                functools.partial(second_kernel, depth=depth, step=step, cells=cells),
                [big, big, small],
                ids,
                x,
                g,
                *everyone(sums),
                scratch=[flux],
            )
            if frame == 0 and sweep == 0:
                (mine,) = call(
                    place_gram_kernel,
                    [((slices * 16, pixels), BF16)],
                    ids,
                    after(plane, sums),
                    *spread,
                )
                other = move(mine, flip(dc=1))
                b_wide[0] = b_rows(quarters)
            if frame == 0 and sweep == 2:
                b_wide[1] = b_rows([after(later[0], x)] + later[1:])
            last = sweep == SWEEPS - 1
            final = last and frame == FRAMES - 1
            outs = [big] + [((slices, pixels), F32)] * last
            if not final:
                outs += [big, small]
            outs = call(
                functools.partial(
                    subset_kernel, depth=depth, step=step + 1, cells=cells, last=last, final=final
                ),
                outs,
                ids,
                x,
                g,
                *everyone(sums),
                mine,
                other,
                *b_wide[frame],
                aux,
                scratch=[flux, pltpu.VMEM((height, pixels), F32)],
            )
            x = outs[0]
            if not final:
                g, sums = outs[-2:]
        local = outs[1]
        passed = move(local, flip(dc=1), keeps)
        finished.append(jnp.where(keeper, local, passed))
    return jnp.stack(finished, axis=0)


def solution(mesh):
    return jax.shard_map(
        body,
        mesh=mesh,
        in_specs=(
            P(None, "view", ("tm", "gz"), None),
            P("view", None, None),
            P(("tm", "gz"), None),
            P(),
        ),
        out_specs=P(None, ("tm", "gz"), None),
        check_vma=False,
    )
```

profile of v0, /device:TPU:0, one launch (start us, length us, event | category | flops | bytes accessed | tf_op | source)
XLA Modules:
  0.0 256.5 jit_solution(7747587240374557626)
XLA Ops:
  0.7 10.6 %gram_products.1 = (f32[4,56,1024]{2,1,0:T(8,128)S(1)}, f32[4,56,1024]{2,1,0:T(8,128)S(1)}) custom-call(s32[10]{0:T(128)S(1)} %concatenate.28.ids_ref, bf16[2,1024,2560]{2,1,0:T(8,128)(2,1)} %a_ref.1, bf16[2,2,64,2560]{3,2,1,0:T(8,128)(2,1)} %s1_ref.1, bf16[2,2,64,2560]{3,2,1,0:T(8,128)(2,1)} %s1_ref.1), custom_call_target="tpu_custom_call" | custom-call | tf_op jit(solution)/shard_map/gram_products/pallas_call | solution.py:158
  11.5 3.2 %collective-permute-start = (f32[64,1024]{1,0:T(8,128)S(1)}, f32[64,1024]{1,0:T(8,128)S(1)}, u32[]{:S(2)}, u32[]{:S(2)}) collective-permute-start(f32[64,1024]{1,0:T(8,128)S(1)} %copy-done), channel_id=1, source_target_pairs={{0,8},{1,9},{2,10},{3,11},{4,12},{5,13},{6,14},{7,15},{8,0},{9,1},... | collective-permute-start | bytes 786440 | tf_op jit(solution)/shard_map/ppermute | solution.py:70
  17.3 3.6 %collective-permute-start.8 = (f32[56,1024]{1,0:T(8,128)S(1)}, f32[56,1024]{1,0:T(8,128)S(1)}, u32[]{:S(2)}, u32[]{:S(2)}) collective-permute-start(f32[56,1024]{1,0:T(8,128)S(1)} %get-tuple-element.70), channel_id=1, source_target_pairs={{0,4},{1,5},{2,6},{3,7},{4,0},{5,1},{6,2},{7,3},{8,12},{9,13},{10,... | collective-permute-start | bytes 688136 | tf_op jit(solution)/shard_map/ppermute | solution.py:70
  21.7 5.2 %collective-permute-start.2 = (f32[2,64,1024]{2,1,0:T(8,128)S(1)}, f32[2,64,1024]{2,1,0:T(8,128)S(1)}, u32[]{:S(2)}, u32[]{:S(2)}) collective-permute-start(f32[2,64,1024]{2,1,0:T(8,128)S(1)} %maximum_select_fusion.1), channel_id=1, source_target_pairs={{0,32},{2,34},{4,36},{6,38},{8,40},{10,42},{12,44},{14,46},{16,48}... | collective-permute-start | bytes 1572872 | tf_op jit(solution)/shard_map/ppermute | solution.py:70
  26.9 2.6 %collective-permute-start.3 = (f32[2,64,1024]{2,1,0:T(8,128)S(1)}, f32[2,64,1024]{2,1,0:T(8,128)S(1)}, u32[]{:S(2)}, u32[]{:S(2)}) collective-permute-start(f32[2,64,1024]{2,1,0:T(8,128)S(1)} %maximum_select_fusion.1), channel_id=1, source_target_pairs={{0,16},{2,18},{4,20},{6,22},{8,24},{10,26},{12,28},{14,30},{16,0},... | collective-permute-start | bytes 1572872 | tf_op jit(solution)/shard_map/ppermute | solution.py:70
  31.5 2.6 %collective-permute-done.9.a3 = f32[56,1024]{1,0:T(8,128)S(1)} collective-permute-done((f32[56,1024]{1,0:T(8,128)S(1)}, f32[56,1024]{1,0:T(8,128)S(1)}, u32[]{:S(2)}, u32[]{:S(2)}) %collective-permute-start.9) | collective-permute-done | bytes 229408 | tf_op jit(solution)/shard_map/ppermute | solution.py:70
  36.6 3.0 %collective-permute-start.22 = (bf16[16,1024]{1,0:T(8,128)(2,1)S(1)}, bf16[16,1024]{1,0:T(8,128)(2,1)S(1)}, u32[]{:S(2)}, u32[]{:S(2)}) collective-permute-start(bf16[16,1024]{1,0:T(8,128)(2,1)S(1)} %get-tuple-element.80), channel_id=1, source_target_pairs={{0,6},{1,7},{2,4},{3,5},{4,2},{5,3},{6,0},{7,1},{8,14},{9,15},{10,... | collective-permute-start | bytes 98312 | tf_op jit(solution)/shard_map/ppermute | solution.py:70
  39.5 4.9 %collective-permute-start.4 = (f32[2,64,1024]{2,1,0:T(8,128)S(1)}, f32[2,64,1024]{2,1,0:T(8,128)S(1)}, u32[]{:S(2)}, u32[]{:S(2)}) collective-permute-start(f32[2,64,1024]{2,1,0:T(8,128)S(1)} %maximum_select_fusion.1), channel_id=1, source_target_pairs={{0,48},{2,50},{4,52},{6,54},{8,56},{10,58},{12,60},{14,62},{16,32}... | collective-permute-start | bytes 1572872 | tf_op jit(solution)/shard_map/ppermute | solution.py:70
  48.2 3.0 %collective-permute-done.10 = f32[2,16,1024]{2,1,0:T(8,128)S(1)} collective-permute-done((f32[2,16,1024]{2,1,0:T(8,128)S(1)}, f32[2,16,1024]{2,1,0:T(8,128)S(1)}, u32[]{:S(2)}, u32[]{:S(2)}) %collective-permute-start.10) | collective-permute-done | bytes 131104 | tf_op jit(solution)/shard_map/ppermute | solution.py:70
  56.1 2.6 %collective-permute-start.11 = (f32[2,2,16,1024]{3,2,1,0:T(8,128)S(1)}, f32[2,2,16,1024]{3,2,1,0:T(8,128)S(1)}, u32[]{:S(2)}, u32[]{:S(2)}) collective-permute-start(f32[2,2,16,1024]{3,2,1,0:T(8,128)S(1)} %maximum_select_fusion.4), channel_id=1, source_target_pairs={{0,32},{2,34},{4,36},{6,38},{8,40},{10,42},{12,44},{14,46},{16,48}... | collective-permute-start | bytes 786440 | tf_op jit(solution)/shard_map/ppermute | solution.py:70
  68.2 4.3 %collective-permute-start.28 = (bf16[16,16,1024]{2,1,0:T(8,128)(2,1)S(1)}, bf16[16,16,1024]{2,1,0:T(8,128)(2,1)S(1)}, u32[]{:S(2)}, u32[]{:S(2)}) collective-permute-start(bf16[16,16,1024]{2,1,0:T(8,128)(2,1)S(1)} %constant_dynamic-update-slice_fusion.y0), channel_id=1, source_target_pairs={{0,48},{1,49},{2,50},{3,51},{4,52},{5,53},{6,54},{7,55},{8,56},{9,... | collective-permute-start | bytes 1572872 | tf_op jit(solution)/shard_map/ppermute | solution.py:70
  74.8 2.7 %collective-permute-start.14 = (f32[8,128]{1,0:T(8,128)S(1)}, f32[8,128]{1,0:T(8,128)S(1)}, u32[]{:S(2)}, u32[]{:S(2)}) collective-permute-start(f32[8,128]{1,0:T(8,128)S(1)} %get-tuple-element.76.s0), channel_id=1, source_target_pairs={{0,1},{1,0},{2,3},{3,2},{4,5},{5,4},{6,7},{7,6},{8,9},{9,8},{10,11... | collective-permute-start | bytes 12296 | tf_op jit(solution)/shard_map/ppermute | solution.py:70
  83.7 6.0 %collective-permute-done.27.y2 = bf16[16,16,1024]{2,1,0:T(8,128)(2,1)S(1)} collective-permute-done((bf16[16,16,1024]{2,1,0:T(8,128)(2,1)S(1)}, bf16[16,16,1024]{2,1,0:T(8,128)(2,1)S(1)}, u32[]{:S(2)}, u32[]{:S(2)}) %collective-permute-start.27) | collective-permute-done | bytes 524320 | tf_op jit(solution)/shard_map/ppermute | solution.py:70
  89.7 4.7 %collective-permute-done.28.y3 = bf16[16,16,1024]{2,1,0:T(8,128)(2,1)S(1)} collective-permute-done((bf16[16,16,1024]{2,1,0:T(8,128)(2,1)S(1)}, bf16[16,16,1024]{2,1,0:T(8,128)(2,1)S(1)}, u32[]{:S(2)}, u32[]{:S(2)}) %collective-permute-start.28) | collective-permute-done | bytes 524320 | tf_op jit(solution)/shard_map/ppermute | solution.py:70
  98.6 2.6 collective-permute-done.54
  103.3 4.9 %collective-permute-done.55 = f32[2,16,1024]{2,1,0:T(8,128)S(1)} collective-permute-done((f32[2,16,1024]{2,1,0:T(8,128)S(1)}, f32[2,16,1024]{2,1,0:T(8,128)S(1)}, u32[]{:S(2)}, u32[]{:S(2)}) %collective-permute-start.55) | collective-permute-done | bytes 131104 | tf_op jit(solution)/shard_map/ppermute | solution.py:70
  110.1 4.3 %collective-permute-start.58 = (f32[2,2,16,1024]{3,2,1,0:T(8,128)S(1)}, f32[2,2,16,1024]{3,2,1,0:T(8,128)S(1)}, u32[]{:S(2)}, u32[]{:S(2)}) collective-permute-start(f32[2,2,16,1024]{3,2,1,0:T(8,128)S(1)} %maximum_select_fusion.5), channel_id=1, source_target_pairs={{0,48},{2,50},{4,52},{6,54},{8,56},{10,58},{12,60},{14,62},{16,32}... | collective-permute-start | bytes 786440 | tf_op jit(solution)/shard_map/ppermute | solution.py:70
  118.0 3.1 %collective-permute-done.58 = f32[2,2,16,1024]{3,2,1,0:T(8,128)S(1)} collective-permute-done((f32[2,2,16,1024]{3,2,1,0:T(8,128)S(1)}, f32[2,2,16,1024]{3,2,1,0:T(8,128)S(1)}, u32[]{:S(2)}, u32[]{:S(2)}) %collective-permute-start.58) | collective-permute-done | bytes 262176 | tf_op jit(solution)/shard_map/ppermute | solution.py:70
  123.2 3.6 %collective-permute-done.18.s2 = f32[8,128]{1,0:T(8,128)S(1)} collective-permute-done((f32[8,128]{1,0:T(8,128)S(1)}, f32[8,128]{1,0:T(8,128)S(1)}, u32[]{:S(2)}, u32[]{:S(2)}) %collective-permute-start.18) | collective-permute-done | bytes 4128 | tf_op jit(solution)/shard_map/ppermute | solution.py:70
  126.8 3.8 %collective-permute-done.30.z1 = f32[4,2,16,1024]{3,2,1,0:T(8,128)S(1)} collective-permute-done((f32[4,2,16,1024]{3,2,1,0:T(8,128)S(1)}, f32[4,2,16,1024]{3,2,1,0:T(8,128)S(1)}, u32[]{:S(2)}, u32[]{:S(2)}) %collective-permute-start.30) | collective-permute-done | bytes 524320 | tf_op jit(solution)/shard_map/ppermute | solution.py:70
  130.8 10.9 %collective-permute-done.31.z2 = f32[4,2,16,1024]{3,2,1,0:T(8,128)S(1)} collective-permute-done((f32[4,2,16,1024]{3,2,1,0:T(8,128)S(1)}, f32[4,2,16,1024]{3,2,1,0:T(8,128)S(1)}, u32[]{:S(2)}, u32[]{:S(2)}) %collective-permute-start.31) | collective-permute-done | bytes 524320 | tf_op jit(solution)/shard_map/ppermute | solution.py:70
  141.6 3.0 %collective-permute-start.61 = (f32[4,2,16,1024]{3,2,1,0:T(8,128)S(1)}, f32[4,2,16,1024]{3,2,1,0:T(8,128)S(1)}, u32[]{:S(2)}, u32[]{:S(2)}) collective-permute-start(f32[4,2,16,1024]{3,2,1,0:T(8,128)S(1)} %maximum_select_fusion.3.z0), channel_id=1, source_target_pairs={{0,6},{1,7},{2,4},{3,5},{4,2},{5,3},{6,0},{7,1},{8,14},{9,15},{10,... | collective-permute-start | bytes 1572872 | tf_op jit(solution)/shard_map/ppermute | solution.py:70
  144.6 3.3 %collective-permute-done.32.z3 = f32[4,2,16,1024]{3,2,1,0:T(8,128)S(1)} collective-permute-done((f32[4,2,16,1024]{3,2,1,0:T(8,128)S(1)}, f32[4,2,16,1024]{3,2,1,0:T(8,128)S(1)}, u32[]{:S(2)}, u32[]{:S(2)}) %collective-permute-start.32) | collective-permute-done | bytes 524320 | tf_op jit(solution)/shard_map/ppermute | solution.py:70
  154.5 3.0 %collective-permute-done.34.high_ref = f32[2,16,1024]{2,1,0:T(8,128)S(1)} collective-permute-done((f32[2,16,1024]{2,1,0:T(8,128)S(1)}, f32[2,16,1024]{2,1,0:T(8,128)S(1)}, u32[]{:S(2)}, u32[]{:S(2)}) %collective-permute-start.34) | collective-permute-done | bytes 131104 | tf_op jit(solution)/shard_map/ppermute | solution.py:70
  157.5 4.7 %shard_map.52 = (f32[288,1024]{1,0:T(8,128)S(1)}, f32[288,1024]{1,0:T(8,128)S(1)}, f32[8,128]{1,0:T(8,128)S(1)}) custom-call(s32[10]{0:T(128)S(1)} %concatenate.28.ids_ref, f32[288,1024]{1,0:T(8,128)S(1)} %get-tuple-element.77.x_ref, f32[288,1024]{1,0:T(8,128)S(1)} %get-tuple-element.78.g_ref, f32[8,128]{1,0:T(8,128)S(1)} %get-tuple-element.79.s0, ...), custom_call_target="tpu_custom_call" | custom-call | tf_op jit(solution)/shard_map/pallas_call | solution.py:41
  162.2 4.6 %collective-permute-start.35 = (f32[8,128]{1,0:T(8,128)S(1)}, f32[8,128]{1,0:T(8,128)S(1)}, u32[]{:S(2)}, u32[]{:S(2)}) collective-permute-start(f32[8,128]{1,0:T(8,128)S(1)} %get-tuple-element.88.s0), channel_id=1, source_target_pairs={{0,1},{1,0},{2,3},{3,2},{4,5},{5,4},{6,7},{7,6},{8,9},{9,8},{10,11... | collective-permute-start | bytes 12296 | tf_op jit(solution)/shard_map/ppermute | solution.py:70
  177.5 4.7 %shard_map.54 = (f32[288,1024]{1,0:T(8,128)S(1)}, f32[288,1024]{1,0:T(8,128)S(1)}, f32[8,128]{1,0:T(8,128)S(1)}) custom-call(s32[10]{0:T(128)S(1)} %concatenate.28.ids_ref, f32[288,1024]{1,0:T(8,128)S(1)} %get-tuple-element.89.x_ref, f32[288,1024]{1,0:T(8,128)S(1)} %get-tuple-element.90.g_ref, f32[8,128]{1,0:T(8,128)S(1)} %get-tuple-element.91.s0, ...), custom_call_target="tpu_custom_call" | custom-call | tf_op jit(solution)/shard_map/pallas_call | solution.py:41
  193.1 4.7 %shard_map.56 = (f32[288,1024]{1,0:T(8,128)S(1)}, f32[64,1024]{1,0:T(8,128)S(1)}, f32[288,1024]{1,0:T(8,128)S(1)}, f32[8,128]{1,0:T(8,128)S(1)}) custom-call(s32[10]{0:T(128)S(1)} %concatenate.28.ids_ref, f32[288,1024]{1,0:T(8,128)S(1)} %get-tuple-element.95.x_ref, f32[288,1024]{1,0:T(8,128)S(1)} %get-tuple-element.96.g_ref, ...), custom_call_target="tpu_custom_call" | custom-call | tf_op jit(solution)/shard_map/pallas_call | solution.py:41
  210.4 2.5 shard_map.57
  217.3 4.7 %shard_map.59 = (f32[288,1024]{1,0:T(8,128)S(1)}, f32[288,1024]{1,0:T(8,128)S(1)}, f32[8,128]{1,0:T(8,128)S(1)}) custom-call(s32[10]{0:T(128)S(1)} %concatenate.28.ids_ref, f32[288,1024]{1,0:T(8,128)S(1)} %get-tuple-element.102.x_ref, f32[288,1024]{1,0:T(8,128)S(1)} %get-tuple-element.103.g_ref, f32[8,128]{1,0:T(8,128)S(1)} %get-tuple-element.104.s0, ...), custom_call_target="tpu_custom_call" | custom-call | tf_op jit(solution)/shard_map/pallas_call | solution.py:41
  232.8 4.7 %shard_map.61 = (f32[288,1024]{1,0:T(8,128)S(1)}, f32[288,1024]{1,0:T(8,128)S(1)}, f32[8,128]{1,0:T(8,128)S(1)}) custom-call(s32[10]{0:T(128)S(1)} %concatenate.28.ids_ref, f32[288,1024]{1,0:T(8,128)S(1)} %get-tuple-element.113.x_ref, f32[288,1024]{1,0:T(8,128)S(1)} %get-tuple-element.114.g_ref, f32[8,128]{1,0:T(8,128)S(1)} %get-tuple-element.115.s0, ...), custom_call_target="tpu_custom_call" | custom-call | tf_op jit(solution)/shard_map/pallas_call | solution.py:41
  248.2 4.2 %shard_map.63 = (f32[288,1024]{1,0:T(8,128)}, f32[64,1024]{1,0:T(8,128)S(1)}) custom-call(s32[10]{0:T(128)S(1)} %concatenate.28.ids_ref, f32[288,1024]{1,0:T(8,128)S(1)} %get-tuple-element.119.x_ref, f32[288,1024]{1,0:T(8,128)S(1)} %get-tuple-element.120.g_ref, f32[8,128]{1,0:T(8,128)S(1)} %get-tuple-element.121.s0, ...), custom_call_target="tpu_custom_call" | custom-call | tf_op jit(solution)/shard_map/pallas_call | solution.py:41
  (169 shorter events, 119.7 us)
Async XLA Ops:
  11.5 10.2 %collective-permute-start = (f32[64,1024]{1,0:T(8,128)S(1)}, f32[64,1024]{1,0:T(8,128)S(1)}, u32[]{:S(2)}, u32[]{:S(2)}) collective-permute-start(f32[64,1024]{1,0:T(8,128)S(1)} %copy-done), channel_id=1, source_target_pairs={{0,8},{1,9},{2,10},{3,11},{4,12},{5,13},{6,14},{7,15},{8,0},{9,1},... | collective-permute-start | bytes 786440 | tf_op jit(solution)/shard_map/ppermute | solution.py:70
  15.3 14.2 %collective-permute-start.7 = (f32[56,1024]{1,0:T(8,128)S(1)}, f32[56,1024]{1,0:T(8,128)S(1)}, u32[]{:S(2)}, u32[]{:S(2)}) collective-permute-start(f32[56,1024]{1,0:T(8,128)S(1)} %get-tuple-element.69), channel_id=1, source_target_pairs={{0,2},{1,3},{2,0},{3,1},{4,6},{5,7},{6,4},{7,5},{8,10},{9,11},{10,... | collective-permute-start | bytes 688136 | tf_op jit(solution)/shard_map/ppermute | solution.py:70
  17.3 14.2 %collective-permute-start.8 = (f32[56,1024]{1,0:T(8,128)S(1)}, f32[56,1024]{1,0:T(8,128)S(1)}, u32[]{:S(2)}, u32[]{:S(2)}) collective-permute-start(f32[56,1024]{1,0:T(8,128)S(1)} %get-tuple-element.70), channel_id=1, source_target_pairs={{0,4},{1,5},{2,6},{3,7},{4,0},{5,1},{6,2},{7,3},{8,12},{9,13},{10,... | collective-permute-start | bytes 688136 | tf_op jit(solution)/shard_map/ppermute | solution.py:70
  20.9 13.2 %collective-permute-start.9 = (f32[56,1024]{1,0:T(8,128)S(1)}, f32[56,1024]{1,0:T(8,128)S(1)}, u32[]{:S(2)}, u32[]{:S(2)}) collective-permute-start(f32[56,1024]{1,0:T(8,128)S(1)} %get-tuple-element.71), channel_id=1, source_target_pairs={{0,6},{1,7},{2,4},{3,5},{4,2},{5,3},{6,0},{7,1},{8,14},{9,15},{10,... | collective-permute-start | bytes 688136 | tf_op jit(solution)/shard_map/ppermute | solution.py:70
  21.7 37.1 %collective-permute-start.2 = (f32[2,64,1024]{2,1,0:T(8,128)S(1)}, f32[2,64,1024]{2,1,0:T(8,128)S(1)}, u32[]{:S(2)}, u32[]{:S(2)}) collective-permute-start(f32[2,64,1024]{2,1,0:T(8,128)S(1)} %maximum_select_fusion.1), channel_id=1, source_target_pairs={{0,32},{2,34},{4,36},{6,38},{8,40},{10,42},{12,44},{14,46},{16,48}... | collective-permute-start | bytes 1572872 | tf_op jit(solution)/shard_map/ppermute | solution.py:70
  26.9 34.3 %collective-permute-start.3 = (f32[2,64,1024]{2,1,0:T(8,128)S(1)}, f32[2,64,1024]{2,1,0:T(8,128)S(1)}, u32[]{:S(2)}, u32[]{:S(2)}) collective-permute-start(f32[2,64,1024]{2,1,0:T(8,128)S(1)} %maximum_select_fusion.1), channel_id=1, source_target_pairs={{0,16},{2,18},{4,20},{6,22},{8,24},{10,26},{12,28},{14,30},{16,0},... | collective-permute-start | bytes 1572872 | tf_op jit(solution)/shard_map/ppermute | solution.py:70
  34.8 9.6 %collective-permute-start.21 = (bf16[16,1024]{1,0:T(8,128)(2,1)S(1)}, bf16[16,1024]{1,0:T(8,128)(2,1)S(1)}, u32[]{:S(2)}, u32[]{:S(2)}) collective-permute-start(bf16[16,1024]{1,0:T(8,128)(2,1)S(1)} %get-tuple-element.80), channel_id=1, source_target_pairs={{0,4},{1,5},{2,6},{3,7},{4,0},{5,1},{6,2},{7,3},{8,12},{9,13},{10,... | collective-permute-start | bytes 98312 | tf_op jit(solution)/shard_map/ppermute | solution.py:70
  36.6 10.4 %collective-permute-start.22 = (bf16[16,1024]{1,0:T(8,128)(2,1)S(1)}, bf16[16,1024]{1,0:T(8,128)(2,1)S(1)}, u32[]{:S(2)}, u32[]{:S(2)}) collective-permute-start(bf16[16,1024]{1,0:T(8,128)(2,1)S(1)} %get-tuple-element.80), channel_id=1, source_target_pairs={{0,6},{1,7},{2,4},{3,5},{4,2},{5,3},{6,0},{7,1},{8,14},{9,15},{10,... | collective-permute-start | bytes 98312 | tf_op jit(solution)/shard_map/ppermute | solution.py:70
  39.5 23.1 %collective-permute-start.4 = (f32[2,64,1024]{2,1,0:T(8,128)S(1)}, f32[2,64,1024]{2,1,0:T(8,128)S(1)}, u32[]{:S(2)}, u32[]{:S(2)}) collective-permute-start(f32[2,64,1024]{2,1,0:T(8,128)S(1)} %maximum_select_fusion.1), channel_id=1, source_target_pairs={{0,48},{2,50},{4,52},{6,54},{8,56},{10,58},{12,60},{14,62},{16,32}... | collective-permute-start | bytes 1572872 | tf_op jit(solution)/shard_map/ppermute | solution.py:70
  44.5 6.7 %collective-permute-start.10 = (f32[2,16,1024]{2,1,0:T(8,128)S(1)}, f32[2,16,1024]{2,1,0:T(8,128)S(1)}, u32[]{:S(2)}, u32[]{:S(2)}) collective-permute-start(f32[2,16,1024]{2,1,0:T(8,128)S(1)} %get-tuple-element.105), channel_id=1, source_target_pairs={{0,8},{1,9},{2,10},{3,11},{4,12},{5,13},{6,14},{7,15},{8,0},{9,1},... | collective-permute-start | bytes 393224 | tf_op jit(solution)/shard_map/ppermute | solution.py:70
  47.0 6.6 %collective-permute-start.23 = (bf16[4,16,1024]{2,1,0:T(8,128)(2,1)S(1)}, bf16[4,16,1024]{2,1,0:T(8,128)(2,1)S(1)}, u32[]{:S(2)}, u32[]{:S(2)}) collective-permute-start(bf16[4,16,1024]{2,1,0:T(8,128)(2,1)S(1)} %pad_maximum_fusion.2), channel_id=1, source_target_pairs={{0,8},{1,9},{2,10},{3,11},{4,12},{5,13},{6,14},{7,15},{8,0},{9,1},... | collective-permute-start | bytes 393224 | tf_op jit(solution)/shard_map/ppermute | solution.py:70
  53.5 10.6 %collective-permute-start.25 = (bf16[4,16,1024]{2,1,0:T(8,128)(2,1)S(1)}, bf16[4,16,1024]{2,1,0:T(8,128)(2,1)S(1)}, u32[]{:S(2)}, u32[]{:S(2)}) collective-permute-start(bf16[4,16,1024]{2,1,0:T(8,128)(2,1)S(1)} %pad_maximum_fusion.2), channel_id=1, source_target_pairs={{0,72},{1,73},{2,74},{3,75},{4,76},{5,77},{6,78},{7,79},{8,64},{9,... | collective-permute-start | bytes 393224 | tf_op jit(solution)/shard_map/ppermute | solution.py:70
  56.1 12.1 %collective-permute-start.11 = (f32[2,2,16,1024]{3,2,1,0:T(8,128)S(1)}, f32[2,2,16,1024]{3,2,1,0:T(8,128)S(1)}, u32[]{:S(2)}, u32[]{:S(2)}) collective-permute-start(f32[2,2,16,1024]{3,2,1,0:T(8,128)S(1)} %maximum_select_fusion.4), channel_id=1, source_target_pairs={{0,32},{2,34},{4,36},{6,38},{8,40},{10,42},{12,44},{14,46},{16,48}... | collective-permute-start | bytes 786440 | tf_op jit(solution)/shard_map/ppermute | solution.py:70
  58.8 13.7 %collective-permute-start.12 = (f32[2,2,16,1024]{3,2,1,0:T(8,128)S(1)}, f32[2,2,16,1024]{3,2,1,0:T(8,128)S(1)}, u32[]{:S(2)}, u32[]{:S(2)}) collective-permute-start(f32[2,2,16,1024]{3,2,1,0:T(8,128)S(1)} %maximum_select_fusion.4), channel_id=1, source_target_pairs={{0,16},{2,18},{4,20},{6,22},{8,24},{10,26},{12,28},{14,30},{16,0},... | collective-permute-start | bytes 786440 | tf_op jit(solution)/shard_map/ppermute | solution.py:70
  61.3 11.3 %collective-permute-start.13 = (f32[2,2,16,1024]{3,2,1,0:T(8,128)S(1)}, f32[2,2,16,1024]{3,2,1,0:T(8,128)S(1)}, u32[]{:S(2)}, u32[]{:S(2)}) collective-permute-start(f32[2,2,16,1024]{3,2,1,0:T(8,128)S(1)} %maximum_select_fusion.4), channel_id=1, source_target_pairs={{0,48},{2,50},{4,52},{6,54},{8,56},{10,58},{12,60},{14,62},{16,32}... | collective-permute-start | bytes 786440 | tf_op jit(solution)/shard_map/ppermute | solution.py:70
  65.4 18.2 %collective-permute-start.26 = (bf16[16,16,1024]{2,1,0:T(8,128)(2,1)S(1)}, bf16[16,16,1024]{2,1,0:T(8,128)(2,1)S(1)}, u32[]{:S(2)}, u32[]{:S(2)}) collective-permute-start(bf16[16,16,1024]{2,1,0:T(8,128)(2,1)S(1)} %constant_dynamic-update-slice_fusion.y0), channel_id=1, source_target_pairs={{0,16},{1,17},{2,18},{3,19},{4,20},{5,21},{6,22},{7,23},{8,24},{9,... | collective-permute-start | bytes 1572872 | tf_op jit(solution)/shard_map/ppermute | solution.py:70
  68.1 21.6 %collective-permute-start.27 = (bf16[16,16,1024]{2,1,0:T(8,128)(2,1)S(1)}, bf16[16,16,1024]{2,1,0:T(8,128)(2,1)S(1)}, u32[]{:S(2)}, u32[]{:S(2)}) collective-permute-start(bf16[16,16,1024]{2,1,0:T(8,128)(2,1)S(1)} %constant_dynamic-update-slice_fusion.y0), channel_id=1, source_target_pairs={{0,32},{1,33},{2,34},{3,35},{4,36},{5,37},{6,38},{7,39},{8,40},{9,... | collective-permute-start | bytes 1572872 | tf_op jit(solution)/shard_map/ppermute | solution.py:70
  68.2 26.2 %collective-permute-start.28 = (bf16[16,16,1024]{2,1,0:T(8,128)(2,1)S(1)}, bf16[16,16,1024]{2,1,0:T(8,128)(2,1)S(1)}, u32[]{:S(2)}, u32[]{:S(2)}) collective-permute-start(bf16[16,16,1024]{2,1,0:T(8,128)(2,1)S(1)} %constant_dynamic-update-slice_fusion.y0), channel_id=1, source_target_pairs={{0,48},{1,49},{2,50},{3,51},{4,52},{5,53},{6,54},{7,55},{8,56},{9,... | collective-permute-start | bytes 1572872 | tf_op jit(solution)/shard_map/ppermute | solution.py:70
  95.3 62.3 %collective-permute-start.29 = (bf16[1024,1024]{1,0:T(8,128)(2,1)S(1)}, bf16[1024,1024]{1,0:T(8,128)(2,1)S(1)}, u32[]{:S(2)}, u32[]{:S(2)}) collective-permute-start(bf16[1024,1024]{1,0:T(8,128)(2,1)S(1)} %shard_map.50.mine_ref), channel_id=1, source_target_pairs={{0,1},{1,0},{2,3},{3,2},{4,5},{5,4},{6,7},{7,6},{8,9},{9,8},{10,11... | collective-permute-start | bytes 6291464 | tf_op jit(solution)/shard_map/ppermute | solution.py:70
  101.1 7.0 %collective-permute-start.55 = (f32[2,16,1024]{2,1,0:T(8,128)S(1)}, f32[2,16,1024]{2,1,0:T(8,128)S(1)}, u32[]{:S(2)}, u32[]{:S(2)}) collective-permute-start(f32[2,16,1024]{2,1,0:T(8,128)S(1)} %collective-permute-done.54), channel_id=1, source_target_pairs={{0,8},{1,9},{2,10},{3,11},{4,12},{5,13},{6,14},{7,15},{8,0},{9,1},... | collective-permute-start | bytes 393224 | tf_op jit(solution)/shard_map/ppermute | solution.py:70
  108.2 8.3 %collective-permute-start.57 = (f32[2,2,16,1024]{3,2,1,0:T(8,128)S(1)}, f32[2,2,16,1024]{3,2,1,0:T(8,128)S(1)}, u32[]{:S(2)}, u32[]{:S(2)}) collective-permute-start(f32[2,2,16,1024]{3,2,1,0:T(8,128)S(1)} %maximum_select_fusion.5), channel_id=1, source_target_pairs={{0,16},{2,18},{4,20},{6,22},{8,24},{10,26},{12,28},{14,30},{16,0},... | collective-permute-start | bytes 786440 | tf_op jit(solution)/shard_map/ppermute | solution.py:70
  110.1 11.0 %collective-permute-start.58 = (f32[2,2,16,1024]{3,2,1,0:T(8,128)S(1)}, f32[2,2,16,1024]{3,2,1,0:T(8,128)S(1)}, u32[]{:S(2)}, u32[]{:S(2)}) collective-permute-start(f32[2,2,16,1024]{3,2,1,0:T(8,128)S(1)} %maximum_select_fusion.5), channel_id=1, source_target_pairs={{0,48},{2,50},{4,52},{6,54},{8,56},{10,58},{12,60},{14,62},{16,32}... | collective-permute-start | bytes 786440 | tf_op jit(solution)/shard_map/ppermute | solution.py:70
  114.4 7.5 %collective-permute-start.56 = (f32[2,2,16,1024]{3,2,1,0:T(8,128)S(1)}, f32[2,2,16,1024]{3,2,1,0:T(8,128)S(1)}, u32[]{:S(2)}, u32[]{:S(2)}) collective-permute-start(f32[2,2,16,1024]{3,2,1,0:T(8,128)S(1)} %maximum_select_fusion.5), channel_id=1, source_target_pairs={{0,32},{2,34},{4,36},{6,38},{8,40},{10,42},{12,44},{14,46},{16,48}... | collective-permute-start | bytes 786440 | tf_op jit(solution)/shard_map/ppermute | solution.py:70
  115.7 14.9 %collective-permute-start.30 = (f32[4,2,16,1024]{3,2,1,0:T(8,128)S(1)}, f32[4,2,16,1024]{3,2,1,0:T(8,128)S(1)}, u32[]{:S(2)}, u32[]{:S(2)}) collective-permute-start(f32[4,2,16,1024]{3,2,1,0:T(8,128)S(1)} %maximum_select_fusion.2.z0), channel_id=1, source_target_pairs={{0,2},{1,3},{2,0},{3,1},{4,6},{5,7},{6,4},{7,5},{8,10},{9,11},{10,... | collective-permute-start | bytes 1572872 | tf_op jit(solution)/shard_map/ppermute | solution.py:70
  116.5 25.2 %collective-permute-start.31 = (f32[4,2,16,1024]{3,2,1,0:T(8,128)S(1)}, f32[4,2,16,1024]{3,2,1,0:T(8,128)S(1)}, u32[]{:S(2)}, u32[]{:S(2)}) collective-permute-start(f32[4,2,16,1024]{3,2,1,0:T(8,128)S(1)} %maximum_select_fusion.2.z0), channel_id=1, source_target_pairs={{0,4},{1,5},{2,6},{3,7},{4,0},{5,1},{6,2},{7,3},{8,12},{9,13},{10,... | collective-permute-start | bytes 1572872 | tf_op jit(solution)/shard_map/ppermute | solution.py:70
  121.1 26.8 %collective-permute-start.32 = (f32[4,2,16,1024]{3,2,1,0:T(8,128)S(1)}, f32[4,2,16,1024]{3,2,1,0:T(8,128)S(1)}, u32[]{:S(2)}, u32[]{:S(2)}) collective-permute-start(f32[4,2,16,1024]{3,2,1,0:T(8,128)S(1)} %maximum_select_fusion.2.z0), channel_id=1, source_target_pairs={{0,6},{1,7},{2,4},{3,5},{4,2},{5,3},{6,0},{7,1},{8,14},{9,15},{10,... | collective-permute-start | bytes 1572872 | tf_op jit(solution)/shard_map/ppermute | solution.py:70
  126.8 73.1 %collective-permute-start.59 = (f32[4,2,16,1024]{3,2,1,0:T(8,128)S(1)}, f32[4,2,16,1024]{3,2,1,0:T(8,128)S(1)}, u32[]{:S(2)}, u32[]{:S(2)}) collective-permute-start(f32[4,2,16,1024]{3,2,1,0:T(8,128)S(1)} %maximum_select_fusion.3.z0), channel_id=1, source_target_pairs={{0,2},{1,3},{2,0},{3,1},{4,6},{5,7},{6,4},{7,5},{8,10},{9,11},{10,... | collective-permute-start | bytes 1572872 | tf_op jit(solution)/shard_map/ppermute | solution.py:70
  130.6 69.3 %collective-permute-start.60 = (f32[4,2,16,1024]{3,2,1,0:T(8,128)S(1)}, f32[4,2,16,1024]{3,2,1,0:T(8,128)S(1)}, u32[]{:S(2)}, u32[]{:S(2)}) collective-permute-start(f32[4,2,16,1024]{3,2,1,0:T(8,128)S(1)} %maximum_select_fusion.3.z0), channel_id=1, source_target_pairs={{0,4},{1,5},{2,6},{3,7},{4,0},{5,1},{6,2},{7,3},{8,12},{9,13},{10,... | collective-permute-start | bytes 1572872 | tf_op jit(solution)/shard_map/ppermute | solution.py:70
  141.6 58.2 %collective-permute-start.61 = (f32[4,2,16,1024]{3,2,1,0:T(8,128)S(1)}, f32[4,2,16,1024]{3,2,1,0:T(8,128)S(1)}, u32[]{:S(2)}, u32[]{:S(2)}) collective-permute-start(f32[4,2,16,1024]{3,2,1,0:T(8,128)S(1)} %maximum_select_fusion.3.z0), channel_id=1, source_target_pairs={{0,6},{1,7},{2,4},{3,5},{4,2},{5,3},{6,0},{7,1},{8,14},{9,15},{10,... | collective-permute-start | bytes 1572872 | tf_op jit(solution)/shard_map/ppermute | solution.py:70
  197.8 56.7 %collective-permute-start.47 = (f32[64,1024]{1,0:T(8,128)S(1)}, f32[64,1024]{1,0:T(8,128)S(1)}, u32[]{:S(2)}, u32[]{:S(2)}) collective-permute-start(f32[64,1024]{1,0:T(8,128)S(1)} %get-tuple-element.98), channel_id=1, source_target_pairs={{0,1},{2,3},{4,5},{6,7},{8,9},{10,11},{12,13},{14,15},{16,17},{18,... | collective-permute-start | bytes 786440 | tf_op jit(solution)/shard_map/ppermute | solution.py:70
  200.6 16.7 %collective-permute-start.62 = (f32[2,16,1024]{2,1,0:T(8,128)S(1)}, f32[2,16,1024]{2,1,0:T(8,128)S(1)}, u32[]{:S(2)}, u32[]{:S(2)}) collective-permute-start(f32[2,16,1024]{2,1,0:T(8,128)S(1)} %get-tuple-element.107), channel_id=1, source_target_pairs={{0,1},{1,64},{2,3},{3,66},{4,5},{5,68},{6,7},{7,70},{8,9},{9,72},{... | collective-permute-start | bytes 393224 | tf_op jit(solution)/shard_map/ppermute | solution.py:70
  201.9 15.4 %collective-permute-start.63 = (f32[2,16,1024]{2,1,0:T(8,128)S(1)}, f32[2,16,1024]{2,1,0:T(8,128)S(1)}, u32[]{:S(2)}, u32[]{:S(2)}) collective-permute-start(f32[2,16,1024]{2,1,0:T(8,128)S(1)} %get-tuple-element.109), channel_id=1, source_target_pairs={{1,0},{3,2},{5,4},{7,6},{9,8},{11,10},{13,12},{15,14},{17,16},{19,... | collective-permute-start | bytes 393224 | tf_op jit(solution)/shard_map/ppermute | solution.py:70
  (46 other events, 152.0 us)
where the time goes:
time: 258 us; the launch traced here: 256 us
  starting transfers between devices  105 us (41%)
  waiting for transfers between devices  90.2 us (35%)
  Pallas kernels  57.9 us (22%)
    ppermute x77, starting transfers between devices, move(): return lax.ppermute(array, AXES, pairs)  105 us
    ppermute x77, waiting for transfers between devices, move(): return lax.ppermute(array, AXES, pairs)  90.2 us
    pallas_call x18, Pallas kernels, call(): pl.pallas_call(kernel, out_shape=tuple((pltpu.VMEM(shape, dtype) for shap...  47.3 us
    pallas_call x1, Pallas kernels, gram_products(): pl.pallas_call(gram_kernel, out_shape=(jax.ShapeDtypeStruct(shape, F32),)...  10.6 us
  transfers between devices with their start and end apart: 77, of which 45 were waited for; matrix products, arithmetic and copies ran while one was open for 0% of the time, Pallas kernels for 18%

commit v1 on v0

--- a/solution.py
+++ b/solution.py
@@ -91,30 +91,34 @@
     rows, det = s0_ref.shape
     my_rows = pl.ds(pl.multiple_of(ids_ref[1] * rows, rows), rows)
 
-    acc[...] = jnp.zeros_like(acc)
-
-    def chunk(d, carry):
-        at = pl.ds(pl.multiple_of(d * CHUNK, CHUNK), CHUNK)
+    def chunk(d, first):
+        at = pl.ds(d * CHUNK, CHUNK) if first else pl.ds(pl.multiple_of(d * CHUNK, CHUNK), CHUNK)
         tile = a_ref[:, at]
         ray = jnp.sum(tile.astype(F32), axis=0, keepdims=True)
         inverse = 1.0 / ray
         lhs = []
         for t, ref in enumerate((s0_ref, s1_ref)):
             scaled = ref[:, at].astype(F32) * inverse
-
-            @pl.when(d == 0)
-            def _():
+            if first:
                 mean = jnp.sum(scaled, axis=1, keepdims=True) / CHUNK
                 level_ref[t] = jnp.broadcast_to(mean, level_ref.shape[1:])
-
             lhs.append((scaled - level_ref[t, :, 0:1]).astype(BF16))
         lhs.append((a_ref[my_rows, at].astype(F32) * inverse).astype(BF16))
         lhs.append(jnp.ones((16, CHUNK), BF16))
         stack = jnp.concatenate(lhs, axis=0)
-        acc[...] += lax.dot_general(stack, tile, (((1,), (1,)), ((), ())), preferred_element_type=F32)
+        product = lax.dot_general(stack, tile, (((1,), (1,)), ((), ())), preferred_element_type=F32)
+        if first:
+            acc[...] = product
+        else:
+            acc[...] += product
+
+    chunk(0, True)
+
+    def further(d, carry):
+        chunk(d, False)
         return carry
 
-    lax.fori_loop(0, det // CHUNK, chunk, 0)
+    lax.fori_loop(1, det // CHUNK, further, 0)
 
     part = rows // QUARTERS
     at = pl.ds(pl.multiple_of(n * part, part), part)

time: 258 us -> 256 us (level)
  transfers between devices with their start and end apart: 77 -> 77, of which waited for: 45 -> 46; matrix products, arithmetic and copies ran while one was open for 0% -> 0% of each run, Pallas kernels for 18% -> 18%
where the time goes in v1:
time: 256 us; the launch traced here: 255 us
  starting transfers between devices  106 us (41%)
  waiting for transfers between devices  90 us (35%)
  Pallas kernels  55.8 us (22%)
    ppermute x77, starting transfers between devices, move(): return lax.ppermute(array, AXES, pairs)  106 us
    ppermute x77, waiting for transfers between devices, move(): return lax.ppermute(array, AXES, pairs)  90 us
    pallas_call x18, Pallas kernels, call(): pl.pallas_call(kernel, out_shape=tuple((pltpu.VMEM(shape, dtype) for shap...  47.1 us
    pallas_call x1, Pallas kernels, gram_products(): pl.pallas_call(gram_kernel, out_shape=(jax.ShapeDtypeStruct(shape, F32),)...  8.69 us
  transfers between devices with their start and end apart: 77, of which 46 were waited for; matrix products, arithmetic and copies ran while one was open for 0% of the time, Pallas kernels for 18%

profile of v1, /device:TPU:0, one launch (start us, length us, event | category | flops | bytes accessed | tf_op | source)
XLA Modules:
  0.0 254.5 jit_solution(13884243623833547597)
XLA Ops:
  0.7 8.7 %gram_products.1 = (f32[4,56,1024]{2,1,0:T(8,128)S(1)}, f32[4,56,1024]{2,1,0:T(8,128)S(1)}) custom-call(s32[10]{0:T(128)S(1)} %concatenate.28.ids_ref, bf16[2,1024,2560]{2,1,0:T(8,128)(2,1)} %a_ref.1, bf16[2,2,64,2560]{3,2,1,0:T(8,128)(2,1)} %s1_ref.1, bf16[2,2,64,2560]{3,2,1,0:T(8,128)(2,1)} %s1_ref.1), custom_call_target="tpu_custom_call" | custom-call | tf_op jit(solution)/shard_map/gram_products/pallas_call | solution.py:162
  9.5 3.2 %collective-permute-start = (f32[64,1024]{1,0:T(8,128)S(1)}, f32[64,1024]{1,0:T(8,128)S(1)}, u32[]{:S(2)}, u32[]{:S(2)}) collective-permute-start(f32[64,1024]{1,0:T(8,128)S(1)} %copy-done), channel_id=1, source_target_pairs={{0,8},{1,9},{2,10},{3,11},{4,12},{5,13},{6,14},{7,15},{8,0},{9,1},... | collective-permute-start | bytes 786440 | tf_op jit(solution)/shard_map/ppermute | solution.py:70
  15.4 3.6 %collective-permute-start.8 = (f32[56,1024]{1,0:T(8,128)S(1)}, f32[56,1024]{1,0:T(8,128)S(1)}, u32[]{:S(2)}, u32[]{:S(2)}) collective-permute-start(f32[56,1024]{1,0:T(8,128)S(1)} %get-tuple-element.70), channel_id=1, source_target_pairs={{0,4},{1,5},{2,6},{3,7},{4,0},{5,1},{6,2},{7,3},{8,12},{9,13},{10,... | collective-permute-start | bytes 688136 | tf_op jit(solution)/shard_map/ppermute | solution.py:70
  19.8 5.3 %collective-permute-start.2 = (f32[2,64,1024]{2,1,0:T(8,128)S(1)}, f32[2,64,1024]{2,1,0:T(8,128)S(1)}, u32[]{:S(2)}, u32[]{:S(2)}) collective-permute-start(f32[2,64,1024]{2,1,0:T(8,128)S(1)} %maximum_select_fusion.1), channel_id=1, source_target_pairs={{0,32},{2,34},{4,36},{6,38},{8,40},{10,42},{12,44},{14,46},{16,48}... | collective-permute-start | bytes 1572872 | tf_op jit(solution)/shard_map/ppermute | solution.py:70
  25.1 2.6 %collective-permute-start.3 = (f32[2,64,1024]{2,1,0:T(8,128)S(1)}, f32[2,64,1024]{2,1,0:T(8,128)S(1)}, u32[]{:S(2)}, u32[]{:S(2)}) collective-permute-start(f32[2,64,1024]{2,1,0:T(8,128)S(1)} %maximum_select_fusion.1), channel_id=1, source_target_pairs={{0,16},{2,18},{4,20},{6,22},{8,24},{10,26},{12,28},{14,30},{16,0},... | collective-permute-start | bytes 1572872 | tf_op jit(solution)/shard_map/ppermute | solution.py:70
  29.6 2.6 %collective-permute-done.9.a3 = f32[56,1024]{1,0:T(8,128)S(1)} collective-permute-done((f32[56,1024]{1,0:T(8,128)S(1)}, f32[56,1024]{1,0:T(8,128)S(1)}, u32[]{:S(2)}, u32[]{:S(2)}) %collective-permute-start.9) | collective-permute-done | bytes 229408 | tf_op jit(solution)/shard_map/ppermute | solution.py:70
  34.7 3.0 %collective-permute-start.22 = (bf16[16,1024]{1,0:T(8,128)(2,1)S(1)}, bf16[16,1024]{1,0:T(8,128)(2,1)S(1)}, u32[]{:S(2)}, u32[]{:S(2)}) collective-permute-start(bf16[16,1024]{1,0:T(8,128)(2,1)S(1)} %get-tuple-element.80), channel_id=1, source_target_pairs={{0,6},{1,7},{2,4},{3,5},{4,2},{5,3},{6,0},{7,1},{8,14},{9,15},{10,... | collective-permute-start | bytes 98312 | tf_op jit(solution)/shard_map/ppermute | solution.py:70
  37.6 5.0 %collective-permute-start.4 = (f32[2,64,1024]{2,1,0:T(8,128)S(1)}, f32[2,64,1024]{2,1,0:T(8,128)S(1)}, u32[]{:S(2)}, u32[]{:S(2)}) collective-permute-start(f32[2,64,1024]{2,1,0:T(8,128)S(1)} %maximum_select_fusion.1), channel_id=1, source_target_pairs={{0,48},{2,50},{4,52},{6,54},{8,56},{10,58},{12,60},{14,62},{16,32}... | collective-permute-start | bytes 1572872 | tf_op jit(solution)/shard_map/ppermute | solution.py:70
  42.6 2.5 collective-permute-start.10
  46.4 2.9 %collective-permute-done.10 = f32[2,16,1024]{2,1,0:T(8,128)S(1)} collective-permute-done((f32[2,16,1024]{2,1,0:T(8,128)S(1)}, f32[2,16,1024]{2,1,0:T(8,128)S(1)}, u32[]{:S(2)}, u32[]{:S(2)}) %collective-permute-start.10) | collective-permute-done | bytes 131104 | tf_op jit(solution)/shard_map/ppermute | solution.py:70
  54.3 2.6 %collective-permute-start.11 = (f32[2,2,16,1024]{3,2,1,0:T(8,128)S(1)}, f32[2,2,16,1024]{3,2,1,0:T(8,128)S(1)}, u32[]{:S(2)}, u32[]{:S(2)}) collective-permute-start(f32[2,2,16,1024]{3,2,1,0:T(8,128)S(1)} %maximum_select_fusion.4), channel_id=1, source_target_pairs={{0,32},{2,34},{4,36},{6,38},{8,40},{10,42},{12,44},{14,46},{16,48}... | collective-permute-start | bytes 786440 | tf_op jit(solution)/shard_map/ppermute | solution.py:70
  66.3 4.3 %collective-permute-start.28 = (bf16[16,16,1024]{2,1,0:T(8,128)(2,1)S(1)}, bf16[16,16,1024]{2,1,0:T(8,128)(2,1)S(1)}, u32[]{:S(2)}, u32[]{:S(2)}) collective-permute-start(bf16[16,16,1024]{2,1,0:T(8,128)(2,1)S(1)} %constant_dynamic-update-slice_fusion.y0), channel_id=1, source_target_pairs={{0,48},{1,49},{2,50},{3,51},{4,52},{5,53},{6,54},{7,55},{8,56},{9,... | collective-permute-start | bytes 1572872 | tf_op jit(solution)/shard_map/ppermute | solution.py:70
  72.8 2.7 %collective-permute-start.14 = (f32[8,128]{1,0:T(8,128)S(1)}, f32[8,128]{1,0:T(8,128)S(1)}, u32[]{:S(2)}, u32[]{:S(2)}) collective-permute-start(f32[8,128]{1,0:T(8,128)S(1)} %get-tuple-element.76.s0), channel_id=1, source_target_pairs={{0,1},{1,0},{2,3},{3,2},{4,5},{5,4},{6,7},{7,6},{8,9},{9,8},{10,11... | collective-permute-start | bytes 12296 | tf_op jit(solution)/shard_map/ppermute | solution.py:70
  81.7 6.1 %collective-permute-done.27.y2 = bf16[16,16,1024]{2,1,0:T(8,128)(2,1)S(1)} collective-permute-done((bf16[16,16,1024]{2,1,0:T(8,128)(2,1)S(1)}, bf16[16,16,1024]{2,1,0:T(8,128)(2,1)S(1)}, u32[]{:S(2)}, u32[]{:S(2)}) %collective-permute-start.27) | collective-permute-done | bytes 524320 | tf_op jit(solution)/shard_map/ppermute | solution.py:70
  87.8 4.7 %collective-permute-done.28.y3 = bf16[16,16,1024]{2,1,0:T(8,128)(2,1)S(1)} collective-permute-done((bf16[16,16,1024]{2,1,0:T(8,128)(2,1)S(1)}, bf16[16,16,1024]{2,1,0:T(8,128)(2,1)S(1)}, u32[]{:S(2)}, u32[]{:S(2)}) %collective-permute-start.28) | collective-permute-done | bytes 524320 | tf_op jit(solution)/shard_map/ppermute | solution.py:70
  96.6 2.6 %collective-permute-done.54 = f32[2,16,1024]{2,1,0:T(8,128)S(1)} collective-permute-done((f32[2,16,1024]{2,1,0:T(8,128)S(1)}, f32[2,16,1024]{2,1,0:T(8,128)S(1)}, u32[]{:S(2)}, u32[]{:S(2)}) %collective-permute-start.54) | collective-permute-done | bytes 131104 | tf_op jit(solution)/shard_map/ppermute | solution.py:70
  101.4 4.9 %collective-permute-done.55 = f32[2,16,1024]{2,1,0:T(8,128)S(1)} collective-permute-done((f32[2,16,1024]{2,1,0:T(8,128)S(1)}, f32[2,16,1024]{2,1,0:T(8,128)S(1)}, u32[]{:S(2)}, u32[]{:S(2)}) %collective-permute-start.55) | collective-permute-done | bytes 131104 | tf_op jit(solution)/shard_map/ppermute | solution.py:70
  108.2 4.3 %collective-permute-start.58 = (f32[2,2,16,1024]{3,2,1,0:T(8,128)S(1)}, f32[2,2,16,1024]{3,2,1,0:T(8,128)S(1)}, u32[]{:S(2)}, u32[]{:S(2)}) collective-permute-start(f32[2,2,16,1024]{3,2,1,0:T(8,128)S(1)} %maximum_select_fusion.5), channel_id=1, source_target_pairs={{0,48},{2,50},{4,52},{6,54},{8,56},{10,58},{12,60},{14,62},{16,32}... | collective-permute-start | bytes 786440 | tf_op jit(solution)/shard_map/ppermute | solution.py:70
  116.1 3.1 %collective-permute-done.58 = f32[2,2,16,1024]{3,2,1,0:T(8,128)S(1)} collective-permute-done((f32[2,2,16,1024]{3,2,1,0:T(8,128)S(1)}, f32[2,2,16,1024]{3,2,1,0:T(8,128)S(1)}, u32[]{:S(2)}, u32[]{:S(2)}) %collective-permute-start.58) | collective-permute-done | bytes 262176 | tf_op jit(solution)/shard_map/ppermute | solution.py:70
  121.5 3.6 %collective-permute-done.18.s2 = f32[8,128]{1,0:T(8,128)S(1)} collective-permute-done((f32[8,128]{1,0:T(8,128)S(1)}, f32[8,128]{1,0:T(8,128)S(1)}, u32[]{:S(2)}, u32[]{:S(2)}) %collective-permute-start.18) | collective-permute-done | bytes 4128 | tf_op jit(solution)/shard_map/ppermute | solution.py:70
  125.0 3.6 %collective-permute-done.30.z1 = f32[4,2,16,1024]{3,2,1,0:T(8,128)S(1)} collective-permute-done((f32[4,2,16,1024]{3,2,1,0:T(8,128)S(1)}, f32[4,2,16,1024]{3,2,1,0:T(8,128)S(1)}, u32[]{:S(2)}, u32[]{:S(2)}) %collective-permute-start.30) | collective-permute-done | bytes 524320 | tf_op jit(solution)/shard_map/ppermute | solution.py:70
  129.0 10.6 %collective-permute-done.31.z2 = f32[4,2,16,1024]{3,2,1,0:T(8,128)S(1)} collective-permute-done((f32[4,2,16,1024]{3,2,1,0:T(8,128)S(1)}, f32[4,2,16,1024]{3,2,1,0:T(8,128)S(1)}, u32[]{:S(2)}, u32[]{:S(2)}) %collective-permute-start.31) | collective-permute-done | bytes 524320 | tf_op jit(solution)/shard_map/ppermute | solution.py:70
  139.6 3.1 %collective-permute-start.61 = (f32[4,2,16,1024]{3,2,1,0:T(8,128)S(1)}, f32[4,2,16,1024]{3,2,1,0:T(8,128)S(1)}, u32[]{:S(2)}, u32[]{:S(2)}) collective-permute-start(f32[4,2,16,1024]{3,2,1,0:T(8,128)S(1)} %maximum_select_fusion.3.z0), channel_id=1, source_target_pairs={{0,6},{1,7},{2,4},{3,5},{4,2},{5,3},{6,0},{7,1},{8,14},{9,15},{10,... | collective-permute-start | bytes 1572872 | tf_op jit(solution)/shard_map/ppermute | solution.py:70
  142.7 3.2 %collective-permute-done.32.z3 = f32[4,2,16,1024]{3,2,1,0:T(8,128)S(1)} collective-permute-done((f32[4,2,16,1024]{3,2,1,0:T(8,128)S(1)}, f32[4,2,16,1024]{3,2,1,0:T(8,128)S(1)}, u32[]{:S(2)}, u32[]{:S(2)}) %collective-permute-start.32) | collective-permute-done | bytes 524320 | tf_op jit(solution)/shard_map/ppermute | solution.py:70
  152.4 3.2 %collective-permute-done.34.high_ref = f32[2,16,1024]{2,1,0:T(8,128)S(1)} collective-permute-done((f32[2,16,1024]{2,1,0:T(8,128)S(1)}, f32[2,16,1024]{2,1,0:T(8,128)S(1)}, u32[]{:S(2)}, u32[]{:S(2)}) %collective-permute-start.34) | collective-permute-done | bytes 131104 | tf_op jit(solution)/shard_map/ppermute | solution.py:70
  155.6 4.7 %shard_map.52 = (f32[288,1024]{1,0:T(8,128)S(1)}, f32[288,1024]{1,0:T(8,128)S(1)}, f32[8,128]{1,0:T(8,128)S(1)}) custom-call(s32[10]{0:T(128)S(1)} %concatenate.28.ids_ref, f32[288,1024]{1,0:T(8,128)S(1)} %get-tuple-element.77.x_ref, f32[288,1024]{1,0:T(8,128)S(1)} %get-tuple-element.78.g_ref, f32[8,128]{1,0:T(8,128)S(1)} %get-tuple-element.79.s0, ...), custom_call_target="tpu_custom_call" | custom-call | tf_op jit(solution)/shard_map/pallas_call | solution.py:41
  160.3 4.6 %collective-permute-start.35 = (f32[8,128]{1,0:T(8,128)S(1)}, f32[8,128]{1,0:T(8,128)S(1)}, u32[]{:S(2)}, u32[]{:S(2)}) collective-permute-start(f32[8,128]{1,0:T(8,128)S(1)} %get-tuple-element.88.s0), channel_id=1, source_target_pairs={{0,1},{1,0},{2,3},{3,2},{4,5},{5,4},{6,7},{7,6},{8,9},{9,8},{10,11... | collective-permute-start | bytes 12296 | tf_op jit(solution)/shard_map/ppermute | solution.py:70
  175.5 4.7 %shard_map.54 = (f32[288,1024]{1,0:T(8,128)S(1)}, f32[288,1024]{1,0:T(8,128)S(1)}, f32[8,128]{1,0:T(8,128)S(1)}) custom-call(s32[10]{0:T(128)S(1)} %concatenate.28.ids_ref, f32[288,1024]{1,0:T(8,128)S(1)} %get-tuple-element.89.x_ref, f32[288,1024]{1,0:T(8,128)S(1)} %get-tuple-element.90.g_ref, f32[8,128]{1,0:T(8,128)S(1)} %get-tuple-element.91.s0, ...), custom_call_target="tpu_custom_call" | custom-call | tf_op jit(solution)/shard_map/pallas_call | solution.py:41
  191.1 4.7 %shard_map.56 = (f32[288,1024]{1,0:T(8,128)S(1)}, f32[64,1024]{1,0:T(8,128)S(1)}, f32[288,1024]{1,0:T(8,128)S(1)}, f32[8,128]{1,0:T(8,128)S(1)}) custom-call(s32[10]{0:T(128)S(1)} %concatenate.28.ids_ref, f32[288,1024]{1,0:T(8,128)S(1)} %get-tuple-element.95.x_ref, f32[288,1024]{1,0:T(8,128)S(1)} %get-tuple-element.96.g_ref, ...), custom_call_target="tpu_custom_call" | custom-call | tf_op jit(solution)/shard_map/pallas_call | solution.py:41
  215.3 4.7 %shard_map.59 = (f32[288,1024]{1,0:T(8,128)S(1)}, f32[288,1024]{1,0:T(8,128)S(1)}, f32[8,128]{1,0:T(8,128)S(1)}) custom-call(s32[10]{0:T(128)S(1)} %concatenate.28.ids_ref, f32[288,1024]{1,0:T(8,128)S(1)} %get-tuple-element.102.x_ref, f32[288,1024]{1,0:T(8,128)S(1)} %get-tuple-element.103.g_ref, f32[8,128]{1,0:T(8,128)S(1)} %get-tuple-element.104.s0, ...), custom_call_target="tpu_custom_call" | custom-call | tf_op jit(solution)/shard_map/pallas_call | solution.py:41
  230.8 4.7 %shard_map.61 = (f32[288,1024]{1,0:T(8,128)S(1)}, f32[288,1024]{1,0:T(8,128)S(1)}, f32[8,128]{1,0:T(8,128)S(1)}) custom-call(s32[10]{0:T(128)S(1)} %concatenate.28.ids_ref, f32[288,1024]{1,0:T(8,128)S(1)} %get-tuple-element.113.x_ref, f32[288,1024]{1,0:T(8,128)S(1)} %get-tuple-element.114.g_ref, f32[8,128]{1,0:T(8,128)S(1)} %get-tuple-element.115.s0, ...), custom_call_target="tpu_custom_call" | custom-call | tf_op jit(solution)/shard_map/pallas_call | solution.py:41
  246.3 4.2 %shard_map.63 = (f32[288,1024]{1,0:T(8,128)}, f32[64,1024]{1,0:T(8,128)S(1)}) custom-call(s32[10]{0:T(128)S(1)} %concatenate.28.ids_ref, f32[288,1024]{1,0:T(8,128)S(1)} %get-tuple-element.119.x_ref, f32[288,1024]{1,0:T(8,128)S(1)} %get-tuple-element.120.g_ref, f32[8,128]{1,0:T(8,128)S(1)} %get-tuple-element.121.s0, ...), custom_call_target="tpu_custom_call" | custom-call | tf_op jit(solution)/shard_map/pallas_call | solution.py:41
  (169 shorter events, 120.0 us)
Async XLA Ops:
  9.5 10.2 %collective-permute-start = (f32[64,1024]{1,0:T(8,128)S(1)}, f32[64,1024]{1,0:T(8,128)S(1)}, u32[]{:S(2)}, u32[]{:S(2)}) collective-permute-start(f32[64,1024]{1,0:T(8,128)S(1)} %copy-done), channel_id=1, source_target_pairs={{0,8},{1,9},{2,10},{3,11},{4,12},{5,13},{6,14},{7,15},{8,0},{9,1},... | collective-permute-start | bytes 786440 | tf_op jit(solution)/shard_map/ppermute | solution.py:70
  13.4 14.3 %collective-permute-start.7 = (f32[56,1024]{1,0:T(8,128)S(1)}, f32[56,1024]{1,0:T(8,128)S(1)}, u32[]{:S(2)}, u32[]{:S(2)}) collective-permute-start(f32[56,1024]{1,0:T(8,128)S(1)} %get-tuple-element.69), channel_id=1, source_target_pairs={{0,2},{1,3},{2,0},{3,1},{4,6},{5,7},{6,4},{7,5},{8,10},{9,11},{10,... | collective-permute-start | bytes 688136 | tf_op jit(solution)/shard_map/ppermute | solution.py:70
  15.4 14.2 %collective-permute-start.8 = (f32[56,1024]{1,0:T(8,128)S(1)}, f32[56,1024]{1,0:T(8,128)S(1)}, u32[]{:S(2)}, u32[]{:S(2)}) collective-permute-start(f32[56,1024]{1,0:T(8,128)S(1)} %get-tuple-element.70), channel_id=1, source_target_pairs={{0,4},{1,5},{2,6},{3,7},{4,0},{5,1},{6,2},{7,3},{8,12},{9,13},{10,... | collective-permute-start | bytes 688136 | tf_op jit(solution)/shard_map/ppermute | solution.py:70
  19.0 13.2 %collective-permute-start.9 = (f32[56,1024]{1,0:T(8,128)S(1)}, f32[56,1024]{1,0:T(8,128)S(1)}, u32[]{:S(2)}, u32[]{:S(2)}) collective-permute-start(f32[56,1024]{1,0:T(8,128)S(1)} %get-tuple-element.71), channel_id=1, source_target_pairs={{0,6},{1,7},{2,4},{3,5},{4,2},{5,3},{6,0},{7,1},{8,14},{9,15},{10,... | collective-permute-start | bytes 688136 | tf_op jit(solution)/shard_map/ppermute | solution.py:70
  19.8 37.1 %collective-permute-start.2 = (f32[2,64,1024]{2,1,0:T(8,128)S(1)}, f32[2,64,1024]{2,1,0:T(8,128)S(1)}, u32[]{:S(2)}, u32[]{:S(2)}) collective-permute-start(f32[2,64,1024]{2,1,0:T(8,128)S(1)} %maximum_select_fusion.1), channel_id=1, source_target_pairs={{0,32},{2,34},{4,36},{6,38},{8,40},{10,42},{12,44},{14,46},{16,48}... | collective-permute-start | bytes 1572872 | tf_op jit(solution)/shard_map/ppermute | solution.py:70
  25.1 34.3 %collective-permute-start.3 = (f32[2,64,1024]{2,1,0:T(8,128)S(1)}, f32[2,64,1024]{2,1,0:T(8,128)S(1)}, u32[]{:S(2)}, u32[]{:S(2)}) collective-permute-start(f32[2,64,1024]{2,1,0:T(8,128)S(1)} %maximum_select_fusion.1), channel_id=1, source_target_pairs={{0,16},{2,18},{4,20},{6,22},{8,24},{10,26},{12,28},{14,30},{16,0},... | collective-permute-start | bytes 1572872 | tf_op jit(solution)/shard_map/ppermute | solution.py:70
  32.9 9.7 %collective-permute-start.21 = (bf16[16,1024]{1,0:T(8,128)(2,1)S(1)}, bf16[16,1024]{1,0:T(8,128)(2,1)S(1)}, u32[]{:S(2)}, u32[]{:S(2)}) collective-permute-start(bf16[16,1024]{1,0:T(8,128)(2,1)S(1)} %get-tuple-element.80), channel_id=1, source_target_pairs={{0,4},{1,5},{2,6},{3,7},{4,0},{5,1},{6,2},{7,3},{8,12},{9,13},{10,... | collective-permute-start | bytes 98312 | tf_op jit(solution)/shard_map/ppermute | solution.py:70
  34.7 10.4 %collective-permute-start.22 = (bf16[16,1024]{1,0:T(8,128)(2,1)S(1)}, bf16[16,1024]{1,0:T(8,128)(2,1)S(1)}, u32[]{:S(2)}, u32[]{:S(2)}) collective-permute-start(bf16[16,1024]{1,0:T(8,128)(2,1)S(1)} %get-tuple-element.80), channel_id=1, source_target_pairs={{0,6},{1,7},{2,4},{3,5},{4,2},{5,3},{6,0},{7,1},{8,14},{9,15},{10,... | collective-permute-start | bytes 98312 | tf_op jit(solution)/shard_map/ppermute | solution.py:70
  37.6 23.1 %collective-permute-start.4 = (f32[2,64,1024]{2,1,0:T(8,128)S(1)}, f32[2,64,1024]{2,1,0:T(8,128)S(1)}, u32[]{:S(2)}, u32[]{:S(2)}) collective-permute-start(f32[2,64,1024]{2,1,0:T(8,128)S(1)} %maximum_select_fusion.1), channel_id=1, source_target_pairs={{0,48},{2,50},{4,52},{6,54},{8,56},{10,58},{12,60},{14,62},{16,32}... | collective-permute-start | bytes 1572872 | tf_op jit(solution)/shard_map/ppermute | solution.py:70
  42.6 6.7 %collective-permute-start.10 = (f32[2,16,1024]{2,1,0:T(8,128)S(1)}, f32[2,16,1024]{2,1,0:T(8,128)S(1)}, u32[]{:S(2)}, u32[]{:S(2)}) collective-permute-start(f32[2,16,1024]{2,1,0:T(8,128)S(1)} %get-tuple-element.105), channel_id=1, source_target_pairs={{0,8},{1,9},{2,10},{3,11},{4,12},{5,13},{6,14},{7,15},{8,0},{9,1},... | collective-permute-start | bytes 393224 | tf_op jit(solution)/shard_map/ppermute | solution.py:70
  45.1 6.6 %collective-permute-start.23 = (bf16[4,16,1024]{2,1,0:T(8,128)(2,1)S(1)}, bf16[4,16,1024]{2,1,0:T(8,128)(2,1)S(1)}, u32[]{:S(2)}, u32[]{:S(2)}) collective-permute-start(bf16[4,16,1024]{2,1,0:T(8,128)(2,1)S(1)} %pad_maximum_fusion.2), channel_id=1, source_target_pairs={{0,8},{1,9},{2,10},{3,11},{4,12},{5,13},{6,14},{7,15},{8,0},{9,1},... | collective-permute-start | bytes 393224 | tf_op jit(solution)/shard_map/ppermute | solution.py:70
  51.7 10.5 %collective-permute-start.25 = (bf16[4,16,1024]{2,1,0:T(8,128)(2,1)S(1)}, bf16[4,16,1024]{2,1,0:T(8,128)(2,1)S(1)}, u32[]{:S(2)}, u32[]{:S(2)}) collective-permute-start(bf16[4,16,1024]{2,1,0:T(8,128)(2,1)S(1)} %pad_maximum_fusion.2), channel_id=1, source_target_pairs={{0,72},{1,73},{2,74},{3,75},{4,76},{5,77},{6,78},{7,79},{8,64},{9,... | collective-permute-start | bytes 393224 | tf_op jit(solution)/shard_map/ppermute | solution.py:70
  54.3 12.0 %collective-permute-start.11 = (f32[2,2,16,1024]{3,2,1,0:T(8,128)S(1)}, f32[2,2,16,1024]{3,2,1,0:T(8,128)S(1)}, u32[]{:S(2)}, u32[]{:S(2)}) collective-permute-start(f32[2,2,16,1024]{3,2,1,0:T(8,128)S(1)} %maximum_select_fusion.4), channel_id=1, source_target_pairs={{0,32},{2,34},{4,36},{6,38},{8,40},{10,42},{12,44},{14,46},{16,48}... | collective-permute-start | bytes 786440 | tf_op jit(solution)/shard_map/ppermute | solution.py:70
  56.9 13.7 %collective-permute-start.12 = (f32[2,2,16,1024]{3,2,1,0:T(8,128)S(1)}, f32[2,2,16,1024]{3,2,1,0:T(8,128)S(1)}, u32[]{:S(2)}, u32[]{:S(2)}) collective-permute-start(f32[2,2,16,1024]{3,2,1,0:T(8,128)S(1)} %maximum_select_fusion.4), channel_id=1, source_target_pairs={{0,16},{2,18},{4,20},{6,22},{8,24},{10,26},{12,28},{14,30},{16,0},... | collective-permute-start | bytes 786440 | tf_op jit(solution)/shard_map/ppermute | solution.py:70
  59.4 11.3 %collective-permute-start.13 = (f32[2,2,16,1024]{3,2,1,0:T(8,128)S(1)}, f32[2,2,16,1024]{3,2,1,0:T(8,128)S(1)}, u32[]{:S(2)}, u32[]{:S(2)}) collective-permute-start(f32[2,2,16,1024]{3,2,1,0:T(8,128)S(1)} %maximum_select_fusion.4), channel_id=1, source_target_pairs={{0,48},{2,50},{4,52},{6,54},{8,56},{10,58},{12,60},{14,62},{16,32}... | collective-permute-start | bytes 786440 | tf_op jit(solution)/shard_map/ppermute | solution.py:70
  63.5 18.2 %collective-permute-start.26 = (bf16[16,16,1024]{2,1,0:T(8,128)(2,1)S(1)}, bf16[16,16,1024]{2,1,0:T(8,128)(2,1)S(1)}, u32[]{:S(2)}, u32[]{:S(2)}) collective-permute-start(bf16[16,16,1024]{2,1,0:T(8,128)(2,1)S(1)} %constant_dynamic-update-slice_fusion.y0), channel_id=1, source_target_pairs={{0,16},{1,17},{2,18},{3,19},{4,20},{5,21},{6,22},{7,23},{8,24},{9,... | collective-permute-start | bytes 1572872 | tf_op jit(solution)/shard_map/ppermute | solution.py:70
  66.2 21.6 %collective-permute-start.27 = (bf16[16,16,1024]{2,1,0:T(8,128)(2,1)S(1)}, bf16[16,16,1024]{2,1,0:T(8,128)(2,1)S(1)}, u32[]{:S(2)}, u32[]{:S(2)}) collective-permute-start(bf16[16,16,1024]{2,1,0:T(8,128)(2,1)S(1)} %constant_dynamic-update-slice_fusion.y0), channel_id=1, source_target_pairs={{0,32},{1,33},{2,34},{3,35},{4,36},{5,37},{6,38},{7,39},{8,40},{9,... | collective-permute-start | bytes 1572872 | tf_op jit(solution)/shard_map/ppermute | solution.py:70
  66.3 26.2 %collective-permute-start.28 = (bf16[16,16,1024]{2,1,0:T(8,128)(2,1)S(1)}, bf16[16,16,1024]{2,1,0:T(8,128)(2,1)S(1)}, u32[]{:S(2)}, u32[]{:S(2)}) collective-permute-start(bf16[16,16,1024]{2,1,0:T(8,128)(2,1)S(1)} %constant_dynamic-update-slice_fusion.y0), channel_id=1, source_target_pairs={{0,48},{1,49},{2,50},{3,51},{4,52},{5,53},{6,54},{7,55},{8,56},{9,... | collective-permute-start | bytes 1572872 | tf_op jit(solution)/shard_map/ppermute | solution.py:70
  93.3 62.3 %collective-permute-start.29 = (bf16[1024,1024]{1,0:T(8,128)(2,1)S(1)}, bf16[1024,1024]{1,0:T(8,128)(2,1)S(1)}, u32[]{:S(2)}, u32[]{:S(2)}) collective-permute-start(bf16[1024,1024]{1,0:T(8,128)(2,1)S(1)} %shard_map.50.mine_ref), channel_id=1, source_target_pairs={{0,1},{1,0},{2,3},{3,2},{4,5},{5,4},{6,7},{7,6},{8,9},{9,8},{10,11... | collective-permute-start | bytes 6291464 | tf_op jit(solution)/shard_map/ppermute | solution.py:70
  99.2 7.0 %collective-permute-start.55 = (f32[2,16,1024]{2,1,0:T(8,128)S(1)}, f32[2,16,1024]{2,1,0:T(8,128)S(1)}, u32[]{:S(2)}, u32[]{:S(2)}) collective-permute-start(f32[2,16,1024]{2,1,0:T(8,128)S(1)} %collective-permute-done.54), channel_id=1, source_target_pairs={{0,8},{1,9},{2,10},{3,11},{4,12},{5,13},{6,14},{7,15},{8,0},{9,1},... | collective-permute-start | bytes 393224 | tf_op jit(solution)/shard_map/ppermute | solution.py:70
  106.3 8.3 %collective-permute-start.57 = (f32[2,2,16,1024]{3,2,1,0:T(8,128)S(1)}, f32[2,2,16,1024]{3,2,1,0:T(8,128)S(1)}, u32[]{:S(2)}, u32[]{:S(2)}) collective-permute-start(f32[2,2,16,1024]{3,2,1,0:T(8,128)S(1)} %maximum_select_fusion.5), channel_id=1, source_target_pairs={{0,16},{2,18},{4,20},{6,22},{8,24},{10,26},{12,28},{14,30},{16,0},... | collective-permute-start | bytes 786440 | tf_op jit(solution)/shard_map/ppermute | solution.py:70
  108.2 11.0 %collective-permute-start.58 = (f32[2,2,16,1024]{3,2,1,0:T(8,128)S(1)}, f32[2,2,16,1024]{3,2,1,0:T(8,128)S(1)}, u32[]{:S(2)}, u32[]{:S(2)}) collective-permute-start(f32[2,2,16,1024]{3,2,1,0:T(8,128)S(1)} %maximum_select_fusion.5), channel_id=1, source_target_pairs={{0,48},{2,50},{4,52},{6,54},{8,56},{10,58},{12,60},{14,62},{16,32}... | collective-permute-start | bytes 786440 | tf_op jit(solution)/shard_map/ppermute | solution.py:70
  112.5 7.5 %collective-permute-start.56 = (f32[2,2,16,1024]{3,2,1,0:T(8,128)S(1)}, f32[2,2,16,1024]{3,2,1,0:T(8,128)S(1)}, u32[]{:S(2)}, u32[]{:S(2)}) collective-permute-start(f32[2,2,16,1024]{3,2,1,0:T(8,128)S(1)} %maximum_select_fusion.5), channel_id=1, source_target_pairs={{0,32},{2,34},{4,36},{6,38},{8,40},{10,42},{12,44},{14,46},{16,48}... | collective-permute-start | bytes 786440 | tf_op jit(solution)/shard_map/ppermute | solution.py:70
  113.8 14.9 %collective-permute-start.30 = (f32[4,2,16,1024]{3,2,1,0:T(8,128)S(1)}, f32[4,2,16,1024]{3,2,1,0:T(8,128)S(1)}, u32[]{:S(2)}, u32[]{:S(2)}) collective-permute-start(f32[4,2,16,1024]{3,2,1,0:T(8,128)S(1)} %maximum_select_fusion.2.z0), channel_id=1, source_target_pairs={{0,2},{1,3},{2,0},{3,1},{4,6},{5,7},{6,4},{7,5},{8,10},{9,11},{10,... | collective-permute-start | bytes 1572872 | tf_op jit(solution)/shard_map/ppermute | solution.py:70
  114.6 25.0 %collective-permute-start.31 = (f32[4,2,16,1024]{3,2,1,0:T(8,128)S(1)}, f32[4,2,16,1024]{3,2,1,0:T(8,128)S(1)}, u32[]{:S(2)}, u32[]{:S(2)}) collective-permute-start(f32[4,2,16,1024]{3,2,1,0:T(8,128)S(1)} %maximum_select_fusion.2.z0), channel_id=1, source_target_pairs={{0,4},{1,5},{2,6},{3,7},{4,0},{5,1},{6,2},{7,3},{8,12},{9,13},{10,... | collective-permute-start | bytes 1572872 | tf_op jit(solution)/shard_map/ppermute | solution.py:70
  119.2 26.7 %collective-permute-start.32 = (f32[4,2,16,1024]{3,2,1,0:T(8,128)S(1)}, f32[4,2,16,1024]{3,2,1,0:T(8,128)S(1)}, u32[]{:S(2)}, u32[]{:S(2)}) collective-permute-start(f32[4,2,16,1024]{3,2,1,0:T(8,128)S(1)} %maximum_select_fusion.2.z0), channel_id=1, source_target_pairs={{0,6},{1,7},{2,4},{3,5},{4,2},{5,3},{6,0},{7,1},{8,14},{9,15},{10,... | collective-permute-start | bytes 1572872 | tf_op jit(solution)/shard_map/ppermute | solution.py:70
  125.0 72.9 %collective-permute-start.59 = (f32[4,2,16,1024]{3,2,1,0:T(8,128)S(1)}, f32[4,2,16,1024]{3,2,1,0:T(8,128)S(1)}, u32[]{:S(2)}, u32[]{:S(2)}) collective-permute-start(f32[4,2,16,1024]{3,2,1,0:T(8,128)S(1)} %maximum_select_fusion.3.z0), channel_id=1, source_target_pairs={{0,2},{1,3},{2,0},{3,1},{4,6},{5,7},{6,4},{7,5},{8,10},{9,11},{10,... | collective-permute-start | bytes 1572872 | tf_op jit(solution)/shard_map/ppermute | solution.py:70
  128.7 69.3 %collective-permute-start.60 = (f32[4,2,16,1024]{3,2,1,0:T(8,128)S(1)}, f32[4,2,16,1024]{3,2,1,0:T(8,128)S(1)}, u32[]{:S(2)}, u32[]{:S(2)}) collective-permute-start(f32[4,2,16,1024]{3,2,1,0:T(8,128)S(1)} %maximum_select_fusion.3.z0), channel_id=1, source_target_pairs={{0,4},{1,5},{2,6},{3,7},{4,0},{5,1},{6,2},{7,3},{8,12},{9,13},{10,... | collective-permute-start | bytes 1572872 | tf_op jit(solution)/shard_map/ppermute | solution.py:70
  139.6 58.4 %collective-permute-start.61 = (f32[4,2,16,1024]{3,2,1,0:T(8,128)S(1)}, f32[4,2,16,1024]{3,2,1,0:T(8,128)S(1)}, u32[]{:S(2)}, u32[]{:S(2)}) collective-permute-start(f32[4,2,16,1024]{3,2,1,0:T(8,128)S(1)} %maximum_select_fusion.3.z0), channel_id=1, source_target_pairs={{0,6},{1,7},{2,4},{3,5},{4,2},{5,3},{6,0},{7,1},{8,14},{9,15},{10,... | collective-permute-start | bytes 1572872 | tf_op jit(solution)/shard_map/ppermute | solution.py:70
  195.8 56.7 %collective-permute-start.47 = (f32[64,1024]{1,0:T(8,128)S(1)}, f32[64,1024]{1,0:T(8,128)S(1)}, u32[]{:S(2)}, u32[]{:S(2)}) collective-permute-start(f32[64,1024]{1,0:T(8,128)S(1)} %get-tuple-element.98), channel_id=1, source_target_pairs={{0,1},{2,3},{4,5},{6,7},{8,9},{10,11},{12,13},{14,15},{16,17},{18,... | collective-permute-start | bytes 786440 | tf_op jit(solution)/shard_map/ppermute | solution.py:70
  198.7 16.6 %collective-permute-start.62 = (f32[2,16,1024]{2,1,0:T(8,128)S(1)}, f32[2,16,1024]{2,1,0:T(8,128)S(1)}, u32[]{:S(2)}, u32[]{:S(2)}) collective-permute-start(f32[2,16,1024]{2,1,0:T(8,128)S(1)} %get-tuple-element.107), channel_id=1, source_target_pairs={{0,1},{1,64},{2,3},{3,66},{4,5},{5,68},{6,7},{7,70},{8,9},{9,72},{... | collective-permute-start | bytes 393224 | tf_op jit(solution)/shard_map/ppermute | solution.py:70
  200.0 15.3 %collective-permute-start.63 = (f32[2,16,1024]{2,1,0:T(8,128)S(1)}, f32[2,16,1024]{2,1,0:T(8,128)S(1)}, u32[]{:S(2)}, u32[]{:S(2)}) collective-permute-start(f32[2,16,1024]{2,1,0:T(8,128)S(1)} %get-tuple-element.109), channel_id=1, source_target_pairs={{1,0},{3,2},{5,4},{7,6},{9,8},{11,10},{13,12},{15,14},{17,16},{19,... | collective-permute-start | bytes 393224 | tf_op jit(solution)/shard_map/ppermute | solution.py:70
  (46 other events, 150.6 us)
